TPU v7x, 32 devices: a whole 2x2x4 slice. The times are simulated.
32 devices in a mesh: outer: 4 (over x, core), inner: 8 (over z, y).
Axes of the slice: x: 2, y: 2, z: 4, core: 2. Of those that a mesh axis runs over, the one named last changes fastest.
Arguments:
- vertex: float32 [131072, 128], P(('outer', 'inner')), may hold values from -1.75 to 1.75
- context: float32 [65536, 128], P(('outer', 'inner')), may hold values from -1.75 to 1.75
- tile_count: int32 [128], P(('outer', 'inner')), may hold values from 1 to 8, as said below
- tile_vert: int32 [128, 8], P(('outer', 'inner')), may hold values from 0 to 15
- tile_context: int32 [128, 8], P(('outer', 'inner')), may hold values from 0 to 7
- positives: int32 [128, 8, 256], P(('outer', 'inner')), may hold values from 0 to 255
- negatives: int32 [128, 8, 4, 256], P(('outer', 'inner')), may hold values from 0 to 255
Outputs:
- vertex_out: float32 [131072, 128], P(('outer', 'inner'))
- context_out: float32 [65536, 128], P(('outer', 'inner'))
Inputs may be any that keep to these rules, and one draw needn't show every extreme that they name: `tile_count`: every entry is at least 1, and in every tour step some device has all 8 slots live.
All inputs are finite; a program needn't handle non-finite values.
Results may differ from a plain program's by a relative error of at most 0.0003.
Values sent between devices are 32-bit elements; how exact they have to be, the bound alone decides.
A program may use at most 64 MiB of HBM per device.

v0:
```python
import functools

import jax
import jax.numpy as jnp
from jax import lax
from jax.experimental import pallas as pl
from jax.experimental.pallas import tpu as pltpu
from jax.sharding import PartitionSpec as P


TILE = 256

learn_rate = 0.5


def halves(x):
    high = x.astype(jnp.bfloat16)
    low = (x - high.astype(jnp.float32)).astype(jnp.bfloat16)
    return high, low


def dot(a, b, dims):
    return lax.dot_general(a, b, (dims, ((), ())), preferred_element_type=jnp.float32)


def ordered(tiles, slots, listed, order, place, mark):
    for k in range(tiles):
        mark[k] = 0
    for t in range(slots):
        mark[listed(t)] = 1
    found = jnp.int32(0)
    marks = [mark[k] for k in range(tiles)]
    total = functools.reduce(lambda x, y: x + y, marks)
    for k in range(tiles):
        at = jnp.where(marks[k] == 1, found, total + k - found)
        found = found + marks[k]
        order[at] = k
        if place is not None:
            place[k] = at


def train(s, count, vert_at, context_at, positives, negatives, v_old, v_new, c_old, c_new):
    rows = lax.broadcasted_iota(jnp.int32, (TILE, TILE), 0)
    slots = positives.shape[1]
    group = 2 if slots % 2 == 0 else 1
    width = v_old.shape[-1]

    def slot_group(g, carry):
        work = []
        for j in range(group):
            t = g * group + j
            live = (t < count).astype(jnp.float32)
            work.append((t, vert_at(t), context_at(t), live))
        anchors = [halves(v_old[w[1]]) for w in work]
        partners = [halves(c_old[w[2]]) for w in work]
        gradients = []
        for (t, _, _, live), (a_high, a_low), (p_high, p_low) in zip(work, anchors, partners):
            both = jnp.concatenate([a_high, a_low], 1)
            twice = jnp.concatenate([p_high, p_high], 1)
            scores = dot(twice, both, ((1,), (1,))) + dot(p_low, a_high, ((1,), (1,)))
            half = -0.5 * learn_rate * live
            step = half * jnp.tanh(0.5 * scores) + half
            gradient = jnp.where(positives[s, pl.ds(t, 1)] == rows, step + learn_rate * live, 0.0)
            for k in range(negatives.shape[2]):
                gradient += jnp.where(negatives[s, t, pl.ds(k, 1)] == rows, step, 0.0)
            gradients.append(halves(gradient))
        for (t, at, to, _), (a_high, a_low), (p_high, p_low), (g_high, g_low) in zip(
            work, anchors, partners, gradients
        ):
            wide = dot(g_high, jnp.concatenate([p_high, p_low], 1), ((0,), (0,)))
            v_new[at] += wide[:, :width] + wide[:, width:] + dot(g_low, p_high, ((0,), (0,)))
            wide = dot(g_high, jnp.concatenate([a_high, a_low], 1), ((1,), (0,)))
            c_new[to] += wide[:, :width] + wide[:, width:] + dot(g_low, a_high, ((1,), (0,)))
        return carry

    lax.fori_loop(0, (count + group - 1) // group, slot_group, 0)


def first_kernel(s, count, vert, context_tiles, positives, negatives, c_old, v_old, c_new, v_new):
    v_new[...] = v_old[...]
    c_new[...] = c_old[...]
    train(
        s, count[s], lambda t: vert[s, t], lambda t: context_tiles[s, t], positives, negatives,
        v_old, v_new, c_old, c_new,
    )


def pack_kernel(s, right, v, plus, minus, order, mark):
    tiles, near = v.shape[0], plus.shape[0]
    ordered(tiles, right.shape[1], lambda t: right[s + 1, t], order, None, mark)
    for k in range(near):
        plus[k] = v[order[k]]
    for k in range(tiles - near):
        minus[k] = v[order[near + k]]


def merge_kernel(s, *refs):
    count, vert, context_tiles, right, left = refs[:5]
    positives, negatives, c_old, plus_in, minus_in, c_new, plus, minus = refs[5:13]
    v_old, v_new, order, mark = refs[13:]
    tiles, near, slots = v_old.shape[0], plus.shape[0], vert.shape[1]
    ordered(tiles, slots, lambda t: left[s - 1, t], order, None, mark)
    for k in range(tiles):
        tile = plus_in[k] if k < near else minus_in[k - near]
        v_old[order[k]] = tile
        v_new[order[k]] = tile
    c_new[...] = c_old[...]
    train(
        s, count[s], lambda t: vert[s, t], lambda t: context_tiles[s, t], positives, negatives,
        v_old, v_new, c_old, c_new,
    )
    ordered(tiles, slots, lambda t: right[s + 1, t], order, None, mark)
    for k in range(near):
        plus[k] = v_new[order[k]]
    for k in range(tiles - near):
        minus[k] = v_new[order[near + k]]


def near_kernel(
    s, tiles, count, vert, context_tiles, positives, negatives, c_old, v_old, c_new, v_new,
    order, mark, place,
):
    ordered(tiles, vert.shape[1], lambda t: vert[s, t], order, place, mark)
    v_new[...] = v_old[...]
    c_new[...] = c_old[...]
    train(
        s, count[s], lambda t: place[vert[s, t]], lambda t: context_tiles[s, t], positives, negatives,
        v_old, v_new, c_old, c_new,
    )


def final_kernel(s, group, plus, minus, out, order, mark):
    near = plus.shape[0]
    ordered(out.shape[0], group.shape[1], lambda t: group[s, t], order, None, mark)
    for k in range(near):
        out[order[k]] = plus[k]
    for k in range(minus.shape[0]):
        out[order[near + k]] = minus[k]


SMEM = pl.BlockSpec(memory_space=pltpu.SMEM)
VMEM = pl.BlockSpec(memory_space=pltpu.VMEM)


def call(kernel, scalars, arrays, outs, scratch=()):
    return pl.pallas_call(
        kernel,
        out_shape=outs,
        in_specs=[SMEM] * len(scalars) + [VMEM] * len(arrays),
        out_specs=jax.tree.map(lambda _: VMEM, outs),
        scratch_shapes=list(scratch),
        compiler_params=pltpu.CompilerParams(vmem_limit_bytes=48 * 1024 * 1024),
        cost_estimate=pl.CostEstimate(flops=2_000_000_000, bytes_accessed=8_000_000, transcendentals=0),
    )(*scalars, *arrays)


def moved(block, by_outer, by_inner):
    outer, inner = lax.axis_size("outer"), lax.axis_size("inner")
    route = [
        (o * inner + i, (o + by_outer) % outer * inner + (i + by_inner) % inner)
        for o in range(outer)
        for i in range(inner)
    ]
    return lax.ppermute(block, ("outer", "inner"), route)


def body(vertex, context, tile_count, tile_vert, tile_context, positives, negatives):
    steps, slots = tile_vert.shape
    width = vertex.shape[1]
    tiles = vertex.shape[0] // TILE
    near = min(slots, tiles)
    far = tiles - near
    f32 = jnp.float32
    near_shape = jax.ShapeDtypeStruct((near, TILE, width), f32)
    far_shape = jax.ShapeDtypeStruct((far, TILE, width), f32)
    full = (tiles, TILE, width)

    live = jnp.arange(slots, dtype=jnp.int32)[None, :] < tile_count[:, None]
    vert = jnp.where(live, tile_vert, tile_vert[:, :1])
    right = moved(vert, 0, -1)
    left = moved(vert, 0, 1)
    group = moved(vert, 1, 0)

    c = context.reshape(-1, TILE, width)
    v = vertex.reshape(full)
    c_shape = jax.ShapeDtypeStruct(c.shape, f32)
    v_shape = jax.ShapeDtypeStruct(full, f32)
    marks = [pltpu.SMEM((tiles,), jnp.int32), pltpu.SMEM((tiles,), jnp.int32)]
    buffers = [pltpu.VMEM(full, f32), pltpu.VMEM(full, f32)]
    part = functools.partial
    lists = [tile_count, vert, tile_context]
    rows = [positives, negatives]

    c, v = call(part(first_kernel, 0), lists, rows + [c, v], (c_shape, v_shape))
    right, left, group, v = lax.optimization_barrier((right, left, group, v))
    plus, minus = call(part(pack_kernel, 0), [right], [v], (near_shape, far_shape), marks)
    for s in range(steps):
        if s % 2 == 0:
            if s > 0:
                c, plus, minus = call(
                    part(merge_kernel, s), lists + [right, left], rows + [c, plus, minus],
                    (c_shape, near_shape, far_shape), buffers + marks,
                )
            plus = moved(plus, 0, 1)
            minus = moved(minus, 0, 2) if s + 2 < steps else moved(minus, 1, 1)
        else:
            c, plus = call(
                part(near_kernel, s, tiles), lists, rows + [c, plus], (c_shape, near_shape),
                marks + marks[:1],
            )
            if s + 1 < steps:
                plus = moved(plus, 0, 1)
            else:
                plus = moved(plus, 1, 0)
    v = call(part(final_kernel, steps - 1), [group], [plus, minus], v_shape, marks)
    return v.reshape(vertex.shape), c.reshape(context.shape)


def solution(mesh):
    return jax.shard_map(
        body,
        mesh=mesh,
        in_specs=(
            P(("outer", "inner"), None),
            P(("outer", "inner"), None),
            P(("outer", "inner")),
            P(("outer", "inner"), None),
            P(("outer", "inner"), None),
            P(("outer", "inner"), None, None),
            P(("outer", "inner"), None, None, None),
        ),
        out_specs=(P(("outer", "inner"), None), P(("outer", "inner"), None)),
        check_vma=False,
    )
```

profile of v0, /device:TPU:0, one launch (start us, length us, event | category | flops | bytes accessed | tf_op | source)
XLA Modules:
  0.0 151.7 jit_solution(2134230460722876397)
XLA Ops:
  0.6 0.8 slice_reduce_fusion
  1.4 0.8 fusion.vert.refs_1_
  2.2 0.5 collective-permute-start.2
  2.7 2.5 %collective-permute-start.1 = (s32[4,8]{1,0:T(4,128)S(1)}, s32[4,8]{1,0:T(4,128)S(1)}, u32[]{:S(2)}, u32[]{:S(2)}) collective-permute-start(s32[4,8]{1,0:T(4,128)S(1)} %fusion.vert.refs_1_), channel_id=1, source_target_pairs={{0,1},{1,2},{2,3},{3,4},{4,5},{5,6},{6,7},{7,0},{8,9},{9,10},{10,1... | collective-permute-start | bytes 392 | tf_op jit(solution)/shard_map/ppermute | solution.py:164
  5.2 3.1 %collective-permute-start = (s32[4,8]{1,0:T(4,128)S(1)}, s32[4,8]{1,0:T(4,128)S(1)}, u32[]{:S(2)}, u32[]{:S(2)}) collective-permute-start(s32[4,8]{1,0:T(4,128)S(1)} %fusion.vert.refs_1_), channel_id=1, source_target_pairs={{0,7},{1,0},{2,1},{3,2},{4,3},{5,4},{6,5},{7,6},{8,15},{9,8},{10,9... | collective-permute-start | bytes 392 | tf_op jit(solution)/shard_map/ppermute | solution.py:164
  8.3 0.7 copy-done
  8.9 1.2 copy-done.2
  10.2 0.9 copy-done.3
  11.1 0.8 copy-done.5
  11.8 0.7 copy-done.7
  12.5 5.8 %shard_map.86 = (f32[8,256,128]{2,1,0:T(8,128)S(1)}, f32[16,256,128]{2,1,0:T(8,128)S(1)}) custom-call(s32[4]{0:T(128)S(1)} %copy-done, s32[4,8]{1,0:T(4,128)S(1)} %fusion.vert.refs_1_, s32[4,8]{1,0:T(4,128)S(1)} %copy-done.7, s32[4,8,256]{2,1,0:T(8,128)S(1)} %copy-done.5, s32[4,8,4,256]{3,2,1,0:T(4,128)S(1)} %copy-done.3, f32[8,256,128]{2,1,0:T(8,128)S(1)} %bitcast.4, ...), custom_call_target="tpu_custom_call" | custom-call | flops 2000000000 | bytes 8000000 | tf_op jit(solution)/shard_map/pallas_call | solution.py:146
  18.3 0.0 collective-permute-done.1.refs_4_
  18.3 0.0 copy-start.1
  18.3 0.0 copy-start.4
  18.4 0.0 copy-start.6
  18.4 0.0 copy-start.8
  18.4 0.8 shard_map.87
  19.1 0.1 collective-permute-start.3
  19.2 0.1 collective-permute-start.5
  19.3 28.6 %collective-permute-done.3.v_old = f32[8,256,128]{2,1,0:T(8,128)S(1)} collective-permute-done((f32[8,256,128]{2,1,0:T(8,128)S(1)}, f32[8,256,128]{2,1,0:T(8,128)S(1)}, u32[]{:S(2)}, u32[]{:S(2)}) %collective-permute-start.3) | collective-permute-done | bytes 1048608 | tf_op jit(solution)/shard_map/ppermute | solution.py:164
  48.0 3.7 %shard_map.88 = (f32[8,256,128]{2,1,0:T(8,128)S(1)}, f32[8,256,128]{2,1,0:T(8,128)S(1)}) custom-call(s32[4]{0:T(128)S(1)} %copy-done.1, s32[4,8]{1,0:T(4,128)S(1)} %fusion.vert.refs_1_, s32[4,8]{1,0:T(4,128)S(1)} %copy-done.8, s32[4,8,256]{2,1,0:T(8,128)S(1)} %copy-done.6, s32[4,8,4,256]{3,2,1,0:T(4,128)S(1)} %copy-done.4, ...), custom_call_target="tpu_custom_call" | custom-call | flops 2000000000 | bytes 8000000 | tf_op jit(solution)/shard_map/pallas_call | solution.py:146
  51.7 0.1 collective-permute-start.4
  51.8 0.0 copy-start.9
  51.8 39.4 %collective-permute-done.4.refs_8_ = f32[8,256,128]{2,1,0:T(8,128)S(1)} collective-permute-done((f32[8,256,128]{2,1,0:T(8,128)S(1)}, f32[8,256,128]{2,1,0:T(8,128)S(1)}, u32[]{:S(2)}, u32[]{:S(2)}) %collective-permute-start.4) | collective-permute-done | bytes 1048608 | tf_op jit(solution)/shard_map/ppermute | solution.py:164
  91.2 5.9 %shard_map.89 = (f32[8,256,128]{2,1,0:T(8,128)S(1)}, f32[8,256,128]{2,1,0:T(8,128)S(1)}, f32[8,256,128]{2,1,0:T(8,128)S(1)}) custom-call(s32[4]{0:T(128)S(1)} %copy-done.1, s32[4,8]{1,0:T(4,128)S(1)} %fusion.vert.refs_1_, s32[4,8]{1,0:T(4,128)S(1)} %copy-done.8, s32[4,8]{1,0:T(4,128)S(1)} %collective-permute-done.right.refs_3_, ...), custom_call_target="tpu_custom_call" | custom-call | flops 2000000000 | bytes 8000000 | tf_op jit(solution)/shard_map/pallas_call | solution.py:146
  97.1 0.1 collective-permute-start.6
  97.1 0.1 collective-permute-start.8
  97.2 32.4 %collective-permute-done.6.v_old = f32[8,256,128]{2,1,0:T(8,128)S(1)} collective-permute-done((f32[8,256,128]{2,1,0:T(8,128)S(1)}, f32[8,256,128]{2,1,0:T(8,128)S(1)}, u32[]{:S(2)}, u32[]{:S(2)}) %collective-permute-start.6) | collective-permute-done | bytes 1048608 | tf_op jit(solution)/shard_map/ppermute | solution.py:164
  129.6 5.7 %shard_map.90 = (f32[8,256,128]{2,1,0:T(8,128)}, f32[8,256,128]{2,1,0:T(8,128)S(1)}) custom-call(s32[4]{0:T(128)S(1)} %copy-done.1, s32[4,8]{1,0:T(4,128)S(1)} %fusion.vert.refs_1_, s32[4,8]{1,0:T(4,128)S(1)} %copy-done.8, s32[4,8,256]{2,1,0:T(8,128)S(1)} %copy-done.6, s32[4,8,4,256]{3,2,1,0:T(4,128)S(1)} %copy-done.4, ...), custom_call_target="tpu_custom_call" | custom-call | flops 2000000000 | bytes 8000000 | tf_op jit(solution)/shard_map/pallas_call | solution.py:146
  135.3 9.1 %collective-permute-done.8.minus = f32[8,256,128]{2,1,0:T(8,128)S(1)} collective-permute-done((f32[8,256,128]{2,1,0:T(8,128)S(1)}, f32[8,256,128]{2,1,0:T(8,128)S(1)}, u32[]{:S(2)}, u32[]{:S(2)}) %collective-permute-start.8) | collective-permute-done | bytes 1048608 | tf_op jit(solution)/shard_map/ppermute | solution.py:164
  144.5 5.1 %collective-permute-done.7.plus = f32[8,256,128]{2,1,0:T(8,128)S(1)} collective-permute-done((f32[8,256,128]{2,1,0:T(8,128)S(1)}, f32[8,256,128]{2,1,0:T(8,128)S(1)}, u32[]{:S(2)}, u32[]{:S(2)}) %collective-permute-start.7) | collective-permute-done | bytes 1048608 | tf_op jit(solution)/shard_map/ppermute | solution.py:164
  149.6 2.1 %shard_map.91 = f32[16,256,128]{2,1,0:T(8,128)} custom-call(s32[4,8]{1,0:T(4,128)S(1)} %collective-permute-done.2.group, f32[8,256,128]{2,1,0:T(8,128)S(1)} %collective-permute-done.7.plus, f32[8,256,128]{2,1,0:T(8,128)S(1)} %collective-permute-done.8.minus), custom_call_target="tpu_custom_call" | custom-call | flops 2000000000 | bytes 8000000 | tf_op jit(solution)/shard_map/pallas_call | solution.py:146
  (14 shorter events, 0.0 us)
Async XLA Ops:
  2.2 16.1 %collective-permute-start.2 = (s32[4,8]{1,0:T(4,128)S(1)}, s32[4,8]{1,0:T(4,128)S(1)}, u32[]{:S(2)}, u32[]{:S(2)}) collective-permute-start(s32[4,8]{1,0:T(4,128)S(1)} %fusion.vert.refs_1_), channel_id=1, source_target_pairs={{0,8},{1,9},{2,10},{3,11},{4,12},{5,13},{6,14},{7,15},{8,16},{9,17... | collective-permute-start | bytes 392 | tf_op jit(solution)/shard_map/ppermute | solution.py:164
  2.7 15.6 %collective-permute-start.1 = (s32[4,8]{1,0:T(4,128)S(1)}, s32[4,8]{1,0:T(4,128)S(1)}, u32[]{:S(2)}, u32[]{:S(2)}) collective-permute-start(s32[4,8]{1,0:T(4,128)S(1)} %fusion.vert.refs_1_), channel_id=1, source_target_pairs={{0,1},{1,2},{2,3},{3,4},{4,5},{5,6},{6,7},{7,0},{8,9},{9,10},{10,1... | collective-permute-start | bytes 392 | tf_op jit(solution)/shard_map/ppermute | solution.py:164
  5.2 13.1 %collective-permute-start = (s32[4,8]{1,0:T(4,128)S(1)}, s32[4,8]{1,0:T(4,128)S(1)}, u32[]{:S(2)}, u32[]{:S(2)}) collective-permute-start(s32[4,8]{1,0:T(4,128)S(1)} %fusion.vert.refs_1_), channel_id=1, source_target_pairs={{0,7},{1,0},{2,1},{3,2},{4,3},{5,4},{6,5},{7,6},{8,15},{9,8},{10,9... | collective-permute-start | bytes 392 | tf_op jit(solution)/shard_map/ppermute | solution.py:164
  8.3 0.7 copy-start
  8.9 1.2 copy-start.2
  10.2 0.9 copy-start.3
  11.1 0.8 copy-start.5
  11.8 0.7 copy-start.7
  18.3 29.6 %copy-start.1 = (s32[4]{0:T(128)S(1)}, s32[4]{0:T(128)}, u32[]{:S(2)}) copy-start(s32[4]{0:T(128)} %count.5) | copy-start | bytes 52
  18.3 29.6 %copy-start.4 = (s32[4,8,4,256]{3,2,1,0:T(4,128)S(1)}, s32[4,8,4,256]{3,2,1,0:T(4,128)}, u32[]{:S(2)}) copy-start(s32[4,8,4,256]{3,2,1,0:T(4,128)} %negatives.5) | copy-start | bytes 393220
  18.4 29.6 %copy-start.6 = (s32[4,8,256]{2,1,0:T(8,128)S(1)}, s32[4,8,256]{2,1,0:T(8,128)}, u32[]{:S(2)}) copy-start(s32[4,8,256]{2,1,0:T(8,128)} %positives.5) | copy-start | bytes 98308
  18.4 29.6 %copy-start.8 = (s32[4,8]{1,0:T(4,128)S(1)}, s32[4,8]{1,0:T(4,128)}, u32[]{:S(2)}) copy-start(s32[4,8]{1,0:T(4,128)} %context_tiles.5) | copy-start | bytes 388
  19.1 28.8 %collective-permute-start.3 = (f32[8,256,128]{2,1,0:T(8,128)S(1)}, f32[8,256,128]{2,1,0:T(8,128)S(1)}, u32[]{:S(2)}, u32[]{:S(2)}) collective-permute-start(f32[8,256,128]{2,1,0:T(8,128)S(1)} %get-tuple-element.23), channel_id=1, source_target_pairs={{0,1},{1,2},{2,3},{3,4},{4,5},{5,6},{6,7},{7,0},{8,9},{9,10},{10,1... | collective-permute-start | bytes 3145736 | tf_op jit(solution)/shard_map/ppermute | solution.py:164
  19.2 32.5 %collective-permute-start.5 = (f32[8,256,128]{2,1,0:T(8,128)S(1)}, f32[8,256,128]{2,1,0:T(8,128)S(1)}, u32[]{:S(2)}, u32[]{:S(2)}) collective-permute-start(f32[8,256,128]{2,1,0:T(8,128)S(1)} %get-tuple-element.26), channel_id=1, source_target_pairs={{0,2},{1,3},{2,4},{3,5},{4,6},{5,7},{6,0},{7,1},{8,10},{9,11},{10,... | collective-permute-start | bytes 3145736 | tf_op jit(solution)/shard_map/ppermute | solution.py:164
  51.7 39.5 %collective-permute-start.4 = (f32[8,256,128]{2,1,0:T(8,128)S(1)}, f32[8,256,128]{2,1,0:T(8,128)S(1)}, u32[]{:S(2)}, u32[]{:S(2)}) collective-permute-start(f32[8,256,128]{2,1,0:T(8,128)S(1)} %get-tuple-element.25), channel_id=1, source_target_pairs={{0,1},{1,2},{2,3},{3,4},{4,5},{5,6},{6,7},{7,0},{8,9},{9,10},{10,1... | collective-permute-start | bytes 3145736 | tf_op jit(solution)/shard_map/ppermute | solution.py:164
  51.8 39.4 %copy-start.9 = (f32[8,256,128]{2,1,0:T(8,128)}, f32[8,256,128]{2,1,0:T(8,128)S(1)}, u32[]{:S(2)}) copy-start(f32[8,256,128]{2,1,0:T(8,128)S(1)} %collective-permute-done.5.refs_9_) | copy-start | bytes 3145732
  97.1 32.6 %collective-permute-start.6 = (f32[8,256,128]{2,1,0:T(8,128)S(1)}, f32[8,256,128]{2,1,0:T(8,128)S(1)}, u32[]{:S(2)}, u32[]{:S(2)}) collective-permute-start(f32[8,256,128]{2,1,0:T(8,128)S(1)} %get-tuple-element.28), channel_id=1, source_target_pairs={{0,1},{1,2},{2,3},{3,4},{4,5},{5,6},{6,7},{7,0},{8,9},{9,10},{10,1... | collective-permute-start | bytes 3145736 | tf_op jit(solution)/shard_map/ppermute | solution.py:164
  97.1 47.3 %collective-permute-start.8 = (f32[8,256,128]{2,1,0:T(8,128)S(1)}, f32[8,256,128]{2,1,0:T(8,128)S(1)}, u32[]{:S(2)}, u32[]{:S(2)}) collective-permute-start(f32[8,256,128]{2,1,0:T(8,128)S(1)} %get-tuple-element.30), channel_id=1, source_target_pairs={{0,9},{1,10},{2,11},{3,12},{4,13},{5,14},{6,15},{7,8},{8,17},{9,18... | collective-permute-start | bytes 3145736 | tf_op jit(solution)/shard_map/ppermute | solution.py:164
  135.3 14.2 %collective-permute-start.7 = (f32[8,256,128]{2,1,0:T(8,128)S(1)}, f32[8,256,128]{2,1,0:T(8,128)S(1)}, u32[]{:S(2)}, u32[]{:S(2)}) collective-permute-start(f32[8,256,128]{2,1,0:T(8,128)S(1)} %get-tuple-element.29), channel_id=1, source_target_pairs={{0,8},{1,9},{2,10},{3,11},{4,12},{5,13},{6,14},{7,15},{8,16},{9,17... | collective-permute-start | bytes 3145736 | tf_op jit(solution)/shard_map/ppermute | solution.py:164
where the time goes:
time: 153 us; the launch traced here: 152 us
  waiting for transfers between devices  115 us (75%)
  Pallas kernels  24 us (16%)
  starting transfers between devices  6.39 us (4%)
  local copies, waits for them, and re-layouts  5.05 us (3%)
    ppermute x9, waiting for transfers between devices, moved(): return lax.ppermute(block, ('outer', 'inner'), route)  115 us
    pallas_call x6, Pallas kernels, call(): pl.pallas_call(kernel, out_shape=outs, in_specs=[SMEM] * len(scalars) + [...  24 us
    ppermute x9, starting transfers between devices, moved(): return lax.ppermute(block, ('outer', 'inner'), route)  6.39 us
    unnamed x20, local copies, waits for them, and re-layouts  4.25 us
  transfers between devices with their start and end apart: 9, of which 5 were waited for; matrix products, arithmetic and copies ran while one was open for 0% of the time, Pallas kernels for 10%

commit v1 on v0

--- a/solution.py
+++ b/solution.py
@@ -27,7 +27,8 @@
     for k in range(tiles):
         mark[k] = 0
     for t in range(slots):
-        mark[listed(t)] = 1
+        tile = listed(t)
+        mark[jnp.where(tile < 0, listed(0), tile)] = 1
     found = jnp.int32(0)
     marks = [mark[k] for k in range(tiles)]
     total = functools.reduce(lambda x, y: x + y, marks)
@@ -50,7 +51,7 @@
         for j in range(group):
             t = g * group + j
             live = (t < count).astype(jnp.float32)
-            work.append((t, vert_at(t), context_at(t), live))
+            work.append((t, vert_at(jnp.where(t < count, t, 0)), context_at(t), live))
         anchors = [halves(v_old[w[1]]) for w in work]
         partners = [halves(c_old[w[2]]) for w in work]
         gradients = []
@@ -76,50 +77,82 @@
     lax.fori_loop(0, (count + group - 1) // group, slot_group, 0)
 
 
-def first_kernel(s, count, vert, context_tiles, positives, negatives, c_old, v_old, c_new, v_new):
+def split(v, order, plus, minus):
+    near = plus.shape[0]
+    for k in range(near):
+        plus[k] = v[order[k]]
+    for k in range(minus.shape[0]):
+        minus[k] = v[order[near + k]]
+
+
+def first_kernel(
+    s, count, vert, context_tiles, right, positives_hbm, negatives_hbm, c_hbm, v_hbm,
+    c_new, plus, minus, positives, negatives, c_old, v_old, v_new, order, mark, sems,
+):
+    copies = [
+        pltpu.make_async_copy(source, target, sems.at[k])
+        for k, (source, target) in enumerate(
+            (
+                (v_hbm, v_old),
+                (c_hbm, c_old),
+                (positives_hbm.at[pl.ds(s, 1)], positives),
+                (negatives_hbm.at[pl.ds(s, 1)], negatives),
+            )
+        )
+    ]
+    for copy in copies:
+        copy.start()
+    ordered(v_old.shape[0], vert.shape[1], lambda t: right[s + 1, t], order, None, mark)
+    for copy in copies:
+        copy.wait()
     v_new[...] = v_old[...]
+    c_new[...] = c_old[...]
+    train(
+        0, count[s], lambda t: vert[s, t], lambda t: context_tiles[s, t], positives, negatives,
+        v_old, v_new, c_old, c_new,
+    )
+    split(v_new, order, plus, minus)
+
+
+def merge_kernel(s, *refs):
+    count, vert, context_tiles, right, left, odd = refs[:6]
+    positives, negatives, c_old, direct, swapped, relayed, minus_in = refs[6:13]
+    c_new, plus, minus, v_old, v_new, order, mark = refs[13:]
+    tiles, near, slots = v_old.shape[0], plus.shape[0], vert.shape[1]
+    first = direct.shape[0]
+    ordered(tiles, slots, lambda t: left[s - 1, t], order, None, mark)
+
+    def put(k, tile):
+        v_old[order[k]] = tile
+        v_new[order[k]] = tile
+
+    for k in range(first):
+        put(k, direct[k])
+    for k in range(near, tiles):
+        put(k, minus_in[k - near])
+
+    @pl.when(odd[0] == 1)
+    def _():
+        for k in range(first, near):
+            put(k, swapped[k - first])
+
+    @pl.when(odd[0] == 0)
+    def _():
+        for k in range(first, near):
+            put(k, relayed[k - first])
+
     c_new[...] = c_old[...]
     train(
         s, count[s], lambda t: vert[s, t], lambda t: context_tiles[s, t], positives, negatives,
         v_old, v_new, c_old, c_new,
     )
-
-
-def pack_kernel(s, right, v, plus, minus, order, mark):
-    tiles, near = v.shape[0], plus.shape[0]
-    ordered(tiles, right.shape[1], lambda t: right[s + 1, t], order, None, mark)
-    for k in range(near):
-        plus[k] = v[order[k]]
-    for k in range(tiles - near):
-        minus[k] = v[order[near + k]]
-
-
-def merge_kernel(s, *refs):
-    count, vert, context_tiles, right, left = refs[:5]
-    positives, negatives, c_old, plus_in, minus_in, c_new, plus, minus = refs[5:13]
-    v_old, v_new, order, mark = refs[13:]
-    tiles, near, slots = v_old.shape[0], plus.shape[0], vert.shape[1]
-    ordered(tiles, slots, lambda t: left[s - 1, t], order, None, mark)
-    for k in range(tiles):
-        tile = plus_in[k] if k < near else minus_in[k - near]
-        v_old[order[k]] = tile
-        v_new[order[k]] = tile
-    c_new[...] = c_old[...]
-    train(
-        s, count[s], lambda t: vert[s, t], lambda t: context_tiles[s, t], positives, negatives,
-        v_old, v_new, c_old, c_new,
-    )
     ordered(tiles, slots, lambda t: right[s + 1, t], order, None, mark)
-    for k in range(near):
-        plus[k] = v_new[order[k]]
-    for k in range(tiles - near):
-        minus[k] = v_new[order[near + k]]
-
-
-def near_kernel(
-    s, tiles, count, vert, context_tiles, positives, negatives, c_old, v_old, c_new, v_new,
-    order, mark, place,
-):
+    split(v_new, order, plus, minus)
+
+
+def near_kernel(s, tiles, *refs):
+    count, vert, context_tiles, positives, negatives, c_old, v_old, c_new = refs[:8]
+    outs, (v_new, order, mark, place) = refs[8:-4], refs[-4:]
     ordered(tiles, vert.shape[1], lambda t: vert[s, t], order, place, mark)
     v_new[...] = v_old[...]
     c_new[...] = c_old[...]
@@ -127,6 +160,10 @@
         s, count[s], lambda t: place[vert[s, t]], lambda t: context_tiles[s, t], positives, negatives,
         v_old, v_new, c_old, c_new,
     )
+    start = 0
+    for out in outs:
+        out[...] = v_new[pl.ds(start, out.shape[0])]
+        start += out.shape[0]
 
 
 def final_kernel(s, group, plus, minus, out, order, mark):
@@ -142,24 +179,29 @@
 VMEM = pl.BlockSpec(memory_space=pltpu.VMEM)
 
 
-def call(kernel, scalars, arrays, outs, scratch=()):
+HBM = pl.BlockSpec(memory_space=pltpu.HBM)
+
+
+def call(kernel, scalars, arrays, outs, scratch=(), space=VMEM, limit=20):
     return pl.pallas_call(
         kernel,
         out_shape=outs,
-        in_specs=[SMEM] * len(scalars) + [VMEM] * len(arrays),
+        in_specs=[SMEM] * len(scalars) + [space] * len(arrays),
         out_specs=jax.tree.map(lambda _: VMEM, outs),
         scratch_shapes=list(scratch),
-        compiler_params=pltpu.CompilerParams(vmem_limit_bytes=48 * 1024 * 1024),
+        compiler_params=pltpu.CompilerParams(vmem_limit_bytes=limit * 1024 * 1024),
         cost_estimate=pl.CostEstimate(flops=2_000_000_000, bytes_accessed=8_000_000, transcendentals=0),
     )(*scalars, *arrays)
 
 
-def moved(block, by_outer, by_inner):
+def moved(block, by_outer, by_inner, taken=lambda i: True):
     outer, inner = lax.axis_size("outer"), lax.axis_size("inner")
+    target = by_inner if callable(by_inner) else lambda i: (i + by_inner) % inner
     route = [
-        (o * inner + i, (o + by_outer) % outer * inner + (i + by_inner) % inner)
+        (o * inner + i, (o + by_outer) % outer * inner + target(i))
         for o in range(outer)
         for i in range(inner)
+        if taken(i)
     ]
     return lax.ppermute(block, ("outer", "inner"), route)
 
@@ -176,10 +218,9 @@
     full = (tiles, TILE, width)
 
     live = jnp.arange(slots, dtype=jnp.int32)[None, :] < tile_count[:, None]
-    vert = jnp.where(live, tile_vert, tile_vert[:, :1])
+    vert = jnp.where(live, tile_vert, -1)
     right = moved(vert, 0, -1)
-    left = moved(vert, 0, 1)
-    group = moved(vert, 1, 0)
+    odd = lax.rem(lax.axis_index("inner"), 2).reshape(1)
 
     c = context.reshape(-1, TILE, width)
     v = vertex.reshape(full)
@@ -191,27 +232,52 @@
     lists = [tile_count, vert, tile_context]
     rows = [positives, negatives]
 
-    c, v = call(part(first_kernel, 0), lists, rows + [c, v], (c_shape, v_shape))
-    right, left, group, v = lax.optimization_barrier((right, left, group, v))
-    plus, minus = call(part(pack_kernel, 0), [right], [v], (near_shape, far_shape), marks)
+    c, plus, minus = call(
+        part(first_kernel, 0), lists + [right], rows + [c, v], (c_shape, near_shape, far_shape),
+        [
+            pltpu.VMEM((1,) + positives.shape[1:], jnp.int32),
+            pltpu.VMEM((1,) + negatives.shape[1:], jnp.int32),
+            pltpu.VMEM(c.shape, f32),
+            pltpu.VMEM(full, f32),
+            pltpu.VMEM(full, f32),
+        ]
+        + marks
+        + [pltpu.SemaphoreType.DMA((4,))],
+        HBM,
+        62,
+    )
+    late, plus = lax.optimization_barrier((vert, plus))
+    near_buffer = [pltpu.VMEM(near_shape.shape, f32)]
+    half = near // 2
+    halves_shape = tuple(
+        jax.ShapeDtypeStruct((size, TILE, width), f32) for size in (half, near - half)
+    )
     for s in range(steps):
         if s % 2 == 0:
             if s > 0:
                 c, plus, minus = call(
-                    part(merge_kernel, s), lists + [right, left], rows + [c, plus, minus],
+                    part(merge_kernel, s), lists + [right, left, odd],
+                    rows + [c, direct, swapped, relayed, minus],
                     (c_shape, near_shape, far_shape), buffers + marks,
                 )
             plus = moved(plus, 0, 1)
             minus = moved(minus, 0, 2) if s + 2 < steps else moved(minus, 1, 1)
+            if s == 0:
+                left = moved(late, 0, 1)
+                group = moved(late, 1, 0)
         else:
-            c, plus = call(
-                part(near_kernel, s, tiles), lists, rows + [c, plus], (c_shape, near_shape),
-                marks + marks[:1],
+            outs = halves_shape if s + 1 < steps else (near_shape,)
+            c, *parts = call(
+                part(near_kernel, s, tiles), lists, rows + [c, plus], (c_shape,) + outs,
+                near_buffer + marks + marks[:1],
             )
             if s + 1 < steps:
-                plus = moved(plus, 0, 1)
+                direct, swapped = parts
+                swapped = moved(swapped, 0, lambda i: i ^ 1)
+                direct = moved(direct, 0, 1)
+                relayed = moved(swapped, 0, 2, lambda i: i % 2 == 0)
             else:
-                plus = moved(plus, 1, 0)
+                plus = moved(parts[0], 1, 0)
     v = call(part(final_kernel, steps - 1), [group], [plus, minus], v_shape, marks)
     return v.reshape(vertex.shape), c.reshape(context.shape)
 

time: 153 us -> 138 us (0.902)
  waiting for transfers between devices: 115 us -> 91.2 us
  starting transfers between devices: 6.39 us -> 13.2 us
  Pallas kernels: 24 us -> 26.2 us
    ppermute x9 -> x11, waiting for transfers between devices: 115 us -> 91.2 us  [moved(): return lax.ppermute(block, ('outer', 'inner'), route)]
    ppermute x9 -> x11, starting transfers between devices: 6.39 us -> 13.2 us  [moved(): return lax.ppermute(block, ('outer', 'inner'), route)]
    pallas_call x6 -> x5, Pallas kernels: 24 us -> 26.2 us  [call(): pl.pallas_call(kernel, out_shape=outs, in_specs=[SMEM] * len(scalars) + [...]
    unnamed x20 -> x24, local copies, waits for them, and re-layouts: 4.25 us -> 4.67 us
  transfers between devices with their start and end apart: 9 -> 11, of which waited for: 5 -> 6; matrix products, arithmetic and copies ran while one was open for 0% -> 0% of each run, Pallas kernels for 10% -> 7%
where the time goes in v1:
time: 138 us; the launch traced here: 137 us
  waiting for transfers between devices  91.2 us (66%)
  Pallas kernels  26.2 us (19%)
  starting transfers between devices  13.2 us (10%)
  local copies, waits for them, and re-layouts  4.67 us (3%)
    ppermute x11, waiting for transfers between devices, moved(): return lax.ppermute(block, ('outer', 'inner'), route)  91.2 us
    pallas_call x5, Pallas kernels, call(): pl.pallas_call(kernel, out_shape=outs, in_specs=[SMEM] * len(scalars) + [...  26.2 us
    ppermute x11, starting transfers between devices, moved(): return lax.ppermute(block, ('outer', 'inner'), route)  13.2 us
    unnamed x24, local copies, waits for them, and re-layouts  4.67 us
  transfers between devices with their start and end apart: 11, of which 6 were waited for; matrix products, arithmetic and copies ran while one was open for 0% of the time, Pallas kernels for 7%

profile of v1, /device:TPU:0, one launch (start us, length us, event | category | flops | bytes accessed | tf_op | source)
XLA Modules:
  0.0 136.8 jit_solution(10583127396315552267)
XLA Ops:
  0.6 0.8 fusion.vert.refs_1_
  1.4 6.0 %collective-permute-start = (s32[4,8]{1,0:T(4,128)S(1)}, s32[4,8]{1,0:T(4,128)S(1)}, u32[]{:S(2)}, u32[]{:S(2)}) collective-permute-start(s32[4,8]{1,0:T(4,128)S(1)} %fusion.vert.refs_1_), channel_id=1, source_target_pairs={{0,7},{1,0},{2,1},{3,2},{4,3},{5,4},{6,5},{7,6},{8,15},{9,8},{10,9... | collective-permute-start | bytes 392 | tf_op jit(solution)/shard_map/ppermute | solution.py:206
  7.4 1.3 collective-permute-done.right.refs_3_
  8.7 0.6 copy-done.7
  9.3 8.8 %shard_map.86 = (f32[8,256,128]{2,1,0:T(8,128)}, f32[8,256,128]{2,1,0:T(8,128)}, f32[8,256,128]{2,1,0:T(8,128)}) custom-call(s32[4]{0:T(128)} %refs_0_.5, s32[4,8]{1,0:T(4,128)} %copy-done, s32[4,8]{1,0:T(4,128)} %refs_2_.5, s32[4,8]{1,0:T(4,128)} %copy-done.7, s32[4,8,256]{2,1,0:T(8,128)} %refs_3_.3, s32[4,8,4,256]{3,2,1,0:T(4,128)} %refs_4_.3, ...), custom_call_target="tpu_custom_call" | custom-call | flops 2000000000 | bytes 8000000 | tf_op jit(solution)/shard_map/pallas_call | solution.py:186
  18.2 0.1 collective-permute-start.3
  18.2 0.1 collective-permute-start.7
  18.3 28.9 %collective-permute-done.3.refs_6_ = f32[8,256,128]{2,1,0:T(8,128)S(1)} collective-permute-done((f32[8,256,128]{2,1,0:T(8,128)}, f32[8,256,128]{2,1,0:T(8,128)S(1)}, u32[]{:S(2)}, u32[]{:S(2)}) %collective-permute-start.3) | collective-permute-done | bytes 1048608 | tf_op jit(solution)/shard_map/ppermute | solution.py:206
  47.2 0.7 copy-done.1
  47.9 1.2 copy-done.11
  49.1 3.8 %shard_map.87 = (f32[8,256,128]{2,1,0:T(8,128)S(1)}, f32[4,256,128]{2,1,0:T(8,128)S(1)}, f32[4,256,128]{2,1,0:T(8,128)S(1)}) custom-call(s32[4]{0:T(128)S(1)} %copy-done.3, s32[4,8]{1,0:T(4,128)S(1)} %copy-done.1, s32[4,8]{1,0:T(4,128)S(1)} %copy-done.6, s32[4,8,256]{2,1,0:T(8,128)S(1)} %copy-done.5, s32[4,8,4,256]{3,2,1,0:T(4,128)S(1)} %copy-done.4, ...), custom_call_target="tpu_custom_call" | custom-call | flops 2000000000 | bytes 8000000 | tf_op jit(solution)/shard_map/pallas_call | solution.py:186
  52.9 0.0 copy-start.9
  52.9 1.0 copy-done.9
  53.9 0.0 collective-permute-start.5
  53.9 2.0 %collective-permute-start.4 = (f32[4,256,128]{2,1,0:T(8,128)S(1)}, f32[4,256,128]{2,1,0:T(8,128)S(1)}, u32[]{:S(2)}, u32[]{:S(2)}) collective-permute-start(f32[4,256,128]{2,1,0:T(8,128)S(1)} %get-tuple-element.20), channel_id=1, source_target_pairs={{0,1},{1,2},{2,3},{3,4},{4,5},{5,6},{6,7},{7,0},{8,9},{9,10},{10,1... | collective-permute-start | bytes 1572872 | tf_op jit(solution)/shard_map/ppermute | solution.py:206
  55.9 8.1 %collective-permute-done.5.refs_10_ = f32[4,256,128]{2,1,0:T(8,128)S(1)} collective-permute-done((f32[4,256,128]{2,1,0:T(8,128)S(1)}, f32[4,256,128]{2,1,0:T(8,128)S(1)}, u32[]{:S(2)}, u32[]{:S(2)}) %collective-permute-start.5) | collective-permute-done | bytes 524320 | tf_op jit(solution)/shard_map/ppermute | solution.py:206
  63.9 1.9 %collective-permute-start.6 = (f32[4,256,128]{2,1,0:T(8,128)S(1)}, f32[4,256,128]{2,1,0:T(8,128)}, u32[]{:S(2)}, u32[]{:S(2)}) collective-permute-start(f32[4,256,128]{2,1,0:T(8,128)S(1)} %collective-permute-done.5.refs_10_), channel_id=1, source_target_pairs={{0,2},{2,4},{4,6},{6,0},{8,10},{10,12},{12,14},{14,8},{16,18},{18,... | collective-permute-start | bytes 1572872 | tf_op jit(solution)/shard_map/ppermute | solution.py:206
  65.9 0.8 collective-permute-start.2
  66.7 10.4 %collective-permute-done.2.refs_4_ = s32[4,8]{1,0:T(4,128)S(1)} collective-permute-done((s32[4,8]{1,0:T(4,128)S(1)}, s32[4,8]{1,0:T(4,128)S(1)}, u32[]{:S(2)}, u32[]{:S(2)}) %collective-permute-start.2) | collective-permute-done | bytes 160 | tf_op jit(solution)/shard_map/ppermute | solution.py:206
  77.2 0.0 collective-permute-done.7.refs_12_
  77.2 0.0 copy-start.10
  77.2 1.2 copy-done.10
  78.4 5.7 %shard_map.88 = (f32[8,256,128]{2,1,0:T(8,128)S(1)}, f32[8,256,128]{2,1,0:T(8,128)S(1)}, f32[8,256,128]{2,1,0:T(8,128)S(1)}) custom-call(s32[4]{0:T(128)S(1)} %copy-done.3, s32[4,8]{1,0:T(4,128)S(1)} %copy-done.2, s32[4,8]{1,0:T(4,128)S(1)} %copy-done.6, s32[4,8]{1,0:T(4,128)S(1)} %copy-done.8, s32[4,8]{1,0:T(4,128)S(1)} %collective-permute-done.2.refs_4_, ...), custom_call_target="tpu_custom_call" | custom-call | flops 2000000000 | bytes 8000000 | tf_op jit(solution)/shard_map/pallas_call | solution.py:186
  84.2 0.1 collective-permute-start.8
  84.2 0.1 collective-permute-start.10
  84.3 30.4 %collective-permute-done.8.refs_6_ = f32[8,256,128]{2,1,0:T(8,128)S(1)} collective-permute-done((f32[8,256,128]{2,1,0:T(8,128)S(1)}, f32[8,256,128]{2,1,0:T(8,128)S(1)}, u32[]{:S(2)}, u32[]{:S(2)}) %collective-permute-start.8) | collective-permute-done | bytes 1048608 | tf_op jit(solution)/shard_map/ppermute | solution.py:206
  114.7 5.7 %shard_map.89 = (f32[8,256,128]{2,1,0:T(8,128)}, f32[8,256,128]{2,1,0:T(8,128)S(1)}) custom-call(s32[4]{0:T(128)S(1)} %copy-done.3, s32[4,8]{1,0:T(4,128)S(1)} %copy-done.2, s32[4,8]{1,0:T(4,128)S(1)} %copy-done.6, s32[4,8,256]{2,1,0:T(8,128)S(1)} %copy-done.5, s32[4,8,4,256]{3,2,1,0:T(4,128)S(1)} %copy-done.4, ...), custom_call_target="tpu_custom_call" | custom-call | flops 2000000000 | bytes 8000000 | tf_op jit(solution)/shard_map/pallas_call | solution.py:186
  120.4 2.1 %collective-permute-start.1 = (s32[4,8]{1,0:T(4,128)S(1)}, s32[4,8]{1,0:T(4,128)S(1)}, u32[]{:S(2)}, u32[]{:S(2)}) collective-permute-start(s32[4,8]{1,0:T(4,128)S(1)} %copy-done.2), channel_id=1, source_target_pairs={{0,8},{1,9},{2,10},{3,11},{4,12},{5,13},{6,14},{7,15},{8,16},{9,17... | collective-permute-start | bytes 392 | tf_op jit(solution)/shard_map/ppermute | solution.py:206
  122.5 12.1 %collective-permute-done.1.group = s32[4,8]{1,0:T(4,128)S(1)} collective-permute-done((s32[4,8]{1,0:T(4,128)S(1)}, s32[4,8]{1,0:T(4,128)S(1)}, u32[]{:S(2)}, u32[]{:S(2)}) %collective-permute-start.1) | collective-permute-done | bytes 160 | tf_op jit(solution)/shard_map/ppermute | solution.py:206
  134.6 0.0 collective-permute-done.10.minus
  134.6 0.0 collective-permute-done.9.plus
  134.6 2.2 %shard_map.90 = f32[16,256,128]{2,1,0:T(8,128)} custom-call(s32[4,8]{1,0:T(4,128)S(1)} %collective-permute-done.1.group, f32[8,256,128]{2,1,0:T(8,128)S(1)} %collective-permute-done.9.plus, f32[8,256,128]{2,1,0:T(8,128)S(1)} %collective-permute-done.10.minus), custom_call_target="tpu_custom_call" | custom-call | flops 2000000000 | bytes 8000000 | tf_op jit(solution)/shard_map/pallas_call | solution.py:186
  (20 shorter events, 0.0 us)
Async XLA Ops:
  1.4 7.3 %copy-start = (s32[4,8]{1,0:T(4,128)}, s32[4,8]{1,0:T(4,128)S(1)}, u32[]{:S(2)}) copy-start(s32[4,8]{1,0:T(4,128)S(1)} %fusion.vert.refs_1_) | copy-start | bytes 388
  1.4 7.3 %collective-permute-start = (s32[4,8]{1,0:T(4,128)S(1)}, s32[4,8]{1,0:T(4,128)S(1)}, u32[]{:S(2)}, u32[]{:S(2)}) collective-permute-start(s32[4,8]{1,0:T(4,128)S(1)} %fusion.vert.refs_1_), channel_id=1, source_target_pairs={{0,7},{1,0},{2,1},{3,2},{4,3},{5,4},{6,5},{7,6},{8,15},{9,8},{10,9... | collective-permute-start | bytes 392 | tf_op jit(solution)/shard_map/ppermute | solution.py:206
  8.7 0.6 copy-start.7
  9.3 37.9 %copy-start.3 = (s32[4]{0:T(128)S(1)}, s32[4]{0:T(128)}, u32[]{:S(2)}) copy-start(s32[4]{0:T(128)} %refs_0_.5) | copy-start | bytes 52
  9.3 37.9 %copy-start.4 = (s32[4,8,4,256]{3,2,1,0:T(4,128)S(1)}, s32[4,8,4,256]{3,2,1,0:T(4,128)}, u32[]{:S(2)}) copy-start(s32[4,8,4,256]{3,2,1,0:T(4,128)} %refs_4_.3) | copy-start | bytes 393220
  9.3 37.9 %copy-start.5 = (s32[4,8,256]{2,1,0:T(8,128)S(1)}, s32[4,8,256]{2,1,0:T(8,128)}, u32[]{:S(2)}) copy-start(s32[4,8,256]{2,1,0:T(8,128)} %refs_3_.3) | copy-start | bytes 98308
  9.3 37.9 %copy-start.6 = (s32[4,8]{1,0:T(4,128)S(1)}, s32[4,8]{1,0:T(4,128)}, u32[]{:S(2)}) copy-start(s32[4,8]{1,0:T(4,128)} %refs_2_.5) | copy-start | bytes 388
  18.2 29.0 %collective-permute-start.3 = (f32[8,256,128]{2,1,0:T(8,128)}, f32[8,256,128]{2,1,0:T(8,128)S(1)}, u32[]{:S(2)}, u32[]{:S(2)}) collective-permute-start(f32[8,256,128]{2,1,0:T(8,128)} %get-tuple-element.18), channel_id=1, source_target_pairs={{0,1},{1,2},{2,3},{3,4},{4,5},{5,6},{6,7},{7,0},{8,9},{9,10},{10,1... | collective-permute-start | bytes 3145736 | tf_op jit(solution)/shard_map/ppermute | solution.py:206
  18.2 58.9 %collective-permute-start.7 = (f32[8,256,128]{2,1,0:T(8,128)}, f32[8,256,128]{2,1,0:T(8,128)S(1)}, u32[]{:S(2)}, u32[]{:S(2)}) collective-permute-start(f32[8,256,128]{2,1,0:T(8,128)} %get-tuple-element.22), channel_id=1, source_target_pairs={{0,2},{1,3},{2,4},{3,5},{4,6},{5,7},{6,0},{7,1},{8,10},{9,11},{10,... | collective-permute-start | bytes 3145736 | tf_op jit(solution)/shard_map/ppermute | solution.py:206
  47.2 0.7 copy-start.1
  47.9 1.2 copy-start.11
  49.1 16.8 %copy-start.2 = (s32[4,8]{1,0:T(4,128)S(1)}, s32[4,8]{1,0:T(4,128)}, u32[]{:S(2)}) copy-start(s32[4,8]{1,0:T(4,128)} %copy-done) | copy-start | bytes 388
  49.1 28.1 %copy-start.8 = (s32[4,8]{1,0:T(4,128)S(1)}, s32[4,8]{1,0:T(4,128)}, u32[]{:S(2)}) copy-start(s32[4,8]{1,0:T(4,128)} %copy-done.7) | copy-start | bytes 388
  52.9 1.0 copy-start.9
  53.9 10.1 %collective-permute-start.5 = (f32[4,256,128]{2,1,0:T(8,128)S(1)}, f32[4,256,128]{2,1,0:T(8,128)S(1)}, u32[]{:S(2)}, u32[]{:S(2)}) collective-permute-start(f32[4,256,128]{2,1,0:T(8,128)S(1)} %get-tuple-element.21), channel_id=1, source_target_pairs={{0,1},{1,0},{2,3},{3,2},{4,5},{5,4},{6,7},{7,6},{8,9},{9,8},{10,11... | collective-permute-start | bytes 1572872 | tf_op jit(solution)/shard_map/ppermute | solution.py:206
  53.9 23.3 %collective-permute-start.4 = (f32[4,256,128]{2,1,0:T(8,128)S(1)}, f32[4,256,128]{2,1,0:T(8,128)S(1)}, u32[]{:S(2)}, u32[]{:S(2)}) collective-permute-start(f32[4,256,128]{2,1,0:T(8,128)S(1)} %get-tuple-element.20), channel_id=1, source_target_pairs={{0,1},{1,2},{2,3},{3,4},{4,5},{5,6},{6,7},{7,0},{8,9},{9,10},{10,1... | collective-permute-start | bytes 1572872 | tf_op jit(solution)/shard_map/ppermute | solution.py:206
  63.9 13.2 %collective-permute-start.6 = (f32[4,256,128]{2,1,0:T(8,128)S(1)}, f32[4,256,128]{2,1,0:T(8,128)}, u32[]{:S(2)}, u32[]{:S(2)}) collective-permute-start(f32[4,256,128]{2,1,0:T(8,128)S(1)} %collective-permute-done.5.refs_10_), channel_id=1, source_target_pairs={{0,2},{2,4},{4,6},{6,0},{8,10},{10,12},{12,14},{14,8},{16,18},{18,... | collective-permute-start | bytes 1572872 | tf_op jit(solution)/shard_map/ppermute | solution.py:206
  65.9 11.3 %collective-permute-start.2 = (s32[4,8]{1,0:T(4,128)S(1)}, s32[4,8]{1,0:T(4,128)S(1)}, u32[]{:S(2)}, u32[]{:S(2)}) collective-permute-start(s32[4,8]{1,0:T(4,128)S(1)} %copy-done.2), channel_id=1, source_target_pairs={{0,1},{1,2},{2,3},{3,4},{4,5},{5,6},{6,7},{7,0},{8,9},{9,10},{10,1... | collective-permute-start | bytes 392 | tf_op jit(solution)/shard_map/ppermute | solution.py:206
  77.2 1.2 copy-start.10
  84.2 30.5 %collective-permute-start.8 = (f32[8,256,128]{2,1,0:T(8,128)S(1)}, f32[8,256,128]{2,1,0:T(8,128)S(1)}, u32[]{:S(2)}, u32[]{:S(2)}) collective-permute-start(f32[8,256,128]{2,1,0:T(8,128)S(1)} %get-tuple-element.24), channel_id=1, source_target_pairs={{0,1},{1,2},{2,3},{3,4},{4,5},{5,6},{6,7},{7,0},{8,9},{9,10},{10,1... | collective-permute-start | bytes 3145736 | tf_op jit(solution)/shard_map/ppermute | solution.py:206
  84.2 50.4 %collective-permute-start.10 = (f32[8,256,128]{2,1,0:T(8,128)S(1)}, f32[8,256,128]{2,1,0:T(8,128)S(1)}, u32[]{:S(2)}, u32[]{:S(2)}) collective-permute-start(f32[8,256,128]{2,1,0:T(8,128)S(1)} %get-tuple-element.26), channel_id=1, source_target_pairs={{0,9},{1,10},{2,11},{3,12},{4,13},{5,14},{6,15},{7,8},{8,17},{9,18... | collective-permute-start | bytes 3145736 | tf_op jit(solution)/shard_map/ppermute | solution.py:206
  120.4 14.3 %collective-permute-start.9 = (f32[8,256,128]{2,1,0:T(8,128)S(1)}, f32[8,256,128]{2,1,0:T(8,128)S(1)}, u32[]{:S(2)}, u32[]{:S(2)}) collective-permute-start(f32[8,256,128]{2,1,0:T(8,128)S(1)} %get-tuple-element.25), channel_id=1, source_target_pairs={{0,8},{1,9},{2,10},{3,11},{4,12},{5,13},{6,14},{7,15},{8,16},{9,17... | collective-permute-start | bytes 3145736 | tf_op jit(solution)/shard_map/ppermute | solution.py:206
  120.4 14.2 %collective-permute-start.1 = (s32[4,8]{1,0:T(4,128)S(1)}, s32[4,8]{1,0:T(4,128)S(1)}, u32[]{:S(2)}, u32[]{:S(2)}) collective-permute-start(s32[4,8]{1,0:T(4,128)S(1)} %copy-done.2), channel_id=1, source_target_pairs={{0,8},{1,9},{2,10},{3,11},{4,12},{5,13},{6,14},{7,15},{8,16},{9,17... | collective-permute-start | bytes 392 | tf_op jit(solution)/shard_map/ppermute | solution.py:206

commit v2 on v1

--- a/solution.py
+++ b/solution.py
@@ -166,13 +166,19 @@
         start += out.shape[0]
 
 
-def final_kernel(s, group, plus, minus, out, order, mark):
-    near = plus.shape[0]
-    ordered(out.shape[0], group.shape[1], lambda t: group[s, t], order, None, mark)
-    for k in range(near):
-        out[order[k]] = plus[k]
-    for k in range(minus.shape[0]):
-        out[order[near + k]] = minus[k]
+def final_kernel(s, group, plus, minus, out, order, mark, sems):
+    near, tiles = plus.shape[0], out.shape[0]
+    ordered(tiles, group.shape[1], lambda t: group[s, t], order, None, mark)
+    copies = [
+        pltpu.make_async_copy(
+            plus.at[k] if k < near else minus.at[k - near], out.at[order[k]], sems.at[k]
+        )
+        for k in range(tiles)
+    ]
+    for copy in copies:
+        copy.start()
+    for copy in copies:
+        copy.wait()
 
 
 SMEM = pl.BlockSpec(memory_space=pltpu.SMEM)
@@ -182,12 +188,12 @@
 HBM = pl.BlockSpec(memory_space=pltpu.HBM)
 
 
-def call(kernel, scalars, arrays, outs, scratch=(), space=VMEM, limit=20):
+def call(kernel, scalars, arrays, outs, scratch=(), space=VMEM, limit=20, out_space=VMEM):
     return pl.pallas_call(
         kernel,
         out_shape=outs,
         in_specs=[SMEM] * len(scalars) + [space] * len(arrays),
-        out_specs=jax.tree.map(lambda _: VMEM, outs),
+        out_specs=jax.tree.map(lambda _: out_space, outs),
         scratch_shapes=list(scratch),
         compiler_params=pltpu.CompilerParams(vmem_limit_bytes=limit * 1024 * 1024),
         cost_estimate=pl.CostEstimate(flops=2_000_000_000, bytes_accessed=8_000_000, transcendentals=0),
@@ -278,7 +284,10 @@
                 relayed = moved(swapped, 0, 2, lambda i: i % 2 == 0)
             else:
                 plus = moved(parts[0], 1, 0)
-    v = call(part(final_kernel, steps - 1), [group], [plus, minus], v_shape, marks)
+    v = call(
+        part(final_kernel, steps - 1), [group], [plus, minus], v_shape,
+        marks + [pltpu.SemaphoreType.DMA((tiles,))], out_space=HBM,
+    )
     return v.reshape(vertex.shape), c.reshape(context.shape)
 
 

time: 138 us -> 138 us (level)
  no operation moved by 1% of the time
where the time goes in v2:
time: 138 us; the launch traced here: 137 us
  waiting for transfers between devices  91.2 us (66%)
  Pallas kernels  26.2 us (19%)
  starting transfers between devices  13.2 us (10%)
  local copies, waits for them, and re-layouts  4.67 us (3%)
    ppermute x11, waiting for transfers between devices, moved(): return lax.ppermute(block, ('outer', 'inner'), route)  91.2 us
    pallas_call x5, Pallas kernels, call(): pl.pallas_call(kernel, out_shape=outs, in_specs=[SMEM] * len(scalars) + [...  26.2 us
    ppermute x11, starting transfers between devices, moved(): return lax.ppermute(block, ('outer', 'inner'), route)  13.2 us
    unnamed x24, local copies, waits for them, and re-layouts  4.67 us
  transfers between devices with their start and end apart: 11, of which 6 were waited for; matrix products, arithmetic and copies ran while one was open for 0% of the time, Pallas kernels for 7%

profile of v2, /device:TPU:0, one launch (start us, length us, event | category | flops | bytes accessed | tf_op | source)
XLA Modules:
  0.0 136.7 jit_solution(13401502404823011700)
XLA Ops:
  0.6 0.8 fusion.vert.refs_1_
  1.4 6.0 %collective-permute-start = (s32[4,8]{1,0:T(4,128)S(1)}, s32[4,8]{1,0:T(4,128)S(1)}, u32[]{:S(2)}, u32[]{:S(2)}) collective-permute-start(s32[4,8]{1,0:T(4,128)S(1)} %fusion.vert.refs_1_), channel_id=1, source_target_pairs={{0,7},{1,0},{2,1},{3,2},{4,3},{5,4},{6,5},{7,6},{8,15},{9,8},{10,9... | collective-permute-start | bytes 392 | tf_op jit(solution)/shard_map/ppermute | solution.py:212
  7.4 1.3 collective-permute-done.right.refs_3_
  8.7 0.6 copy-done.7
  9.3 8.8 %shard_map.86 = (f32[8,256,128]{2,1,0:T(8,128)}, f32[8,256,128]{2,1,0:T(8,128)}, f32[8,256,128]{2,1,0:T(8,128)}) custom-call(s32[4]{0:T(128)} %refs_0_.5, s32[4,8]{1,0:T(4,128)} %copy-done, s32[4,8]{1,0:T(4,128)} %refs_2_.5, s32[4,8]{1,0:T(4,128)} %copy-done.7, s32[4,8,256]{2,1,0:T(8,128)} %refs_3_.3, s32[4,8,4,256]{3,2,1,0:T(4,128)} %refs_4_.3, ...), custom_call_target="tpu_custom_call" | custom-call | flops 2000000000 | bytes 8000000 | tf_op jit(solution)/shard_map/pallas_call | solution.py:192
  18.2 0.1 collective-permute-start.3
  18.2 0.1 collective-permute-start.7
  18.3 28.9 %collective-permute-done.3.refs_6_ = f32[8,256,128]{2,1,0:T(8,128)S(1)} collective-permute-done((f32[8,256,128]{2,1,0:T(8,128)}, f32[8,256,128]{2,1,0:T(8,128)S(1)}, u32[]{:S(2)}, u32[]{:S(2)}) %collective-permute-start.3) | collective-permute-done | bytes 1048608 | tf_op jit(solution)/shard_map/ppermute | solution.py:212
  47.2 0.7 copy-done.1
  47.9 1.2 copy-done.11
  49.1 3.8 %shard_map.87 = (f32[8,256,128]{2,1,0:T(8,128)S(1)}, f32[4,256,128]{2,1,0:T(8,128)S(1)}, f32[4,256,128]{2,1,0:T(8,128)S(1)}) custom-call(s32[4]{0:T(128)S(1)} %copy-done.3, s32[4,8]{1,0:T(4,128)S(1)} %copy-done.1, s32[4,8]{1,0:T(4,128)S(1)} %copy-done.6, s32[4,8,256]{2,1,0:T(8,128)S(1)} %copy-done.5, s32[4,8,4,256]{3,2,1,0:T(4,128)S(1)} %copy-done.4, ...), custom_call_target="tpu_custom_call" | custom-call | flops 2000000000 | bytes 8000000 | tf_op jit(solution)/shard_map/pallas_call | solution.py:192
  52.9 0.0 copy-start.9
  52.9 1.0 copy-done.9
  53.9 0.0 collective-permute-start.5
  53.9 2.0 %collective-permute-start.4 = (f32[4,256,128]{2,1,0:T(8,128)S(1)}, f32[4,256,128]{2,1,0:T(8,128)S(1)}, u32[]{:S(2)}, u32[]{:S(2)}) collective-permute-start(f32[4,256,128]{2,1,0:T(8,128)S(1)} %get-tuple-element.20), channel_id=1, source_target_pairs={{0,1},{1,2},{2,3},{3,4},{4,5},{5,6},{6,7},{7,0},{8,9},{9,10},{10,1... | collective-permute-start | bytes 1572872 | tf_op jit(solution)/shard_map/ppermute | solution.py:212
  55.9 8.1 %collective-permute-done.5.refs_10_ = f32[4,256,128]{2,1,0:T(8,128)S(1)} collective-permute-done((f32[4,256,128]{2,1,0:T(8,128)S(1)}, f32[4,256,128]{2,1,0:T(8,128)S(1)}, u32[]{:S(2)}, u32[]{:S(2)}) %collective-permute-start.5) | collective-permute-done | bytes 524320 | tf_op jit(solution)/shard_map/ppermute | solution.py:212
  63.9 1.9 %collective-permute-start.6 = (f32[4,256,128]{2,1,0:T(8,128)S(1)}, f32[4,256,128]{2,1,0:T(8,128)}, u32[]{:S(2)}, u32[]{:S(2)}) collective-permute-start(f32[4,256,128]{2,1,0:T(8,128)S(1)} %collective-permute-done.5.refs_10_), channel_id=1, source_target_pairs={{0,2},{2,4},{4,6},{6,0},{8,10},{10,12},{12,14},{14,8},{16,18},{18,... | collective-permute-start | bytes 1572872 | tf_op jit(solution)/shard_map/ppermute | solution.py:212
  65.9 0.8 collective-permute-start.2
  66.7 10.4 %collective-permute-done.2.refs_4_ = s32[4,8]{1,0:T(4,128)S(1)} collective-permute-done((s32[4,8]{1,0:T(4,128)S(1)}, s32[4,8]{1,0:T(4,128)S(1)}, u32[]{:S(2)}, u32[]{:S(2)}) %collective-permute-start.2) | collective-permute-done | bytes 160 | tf_op jit(solution)/shard_map/ppermute | solution.py:212
  77.2 0.0 collective-permute-done.7.refs_12_
  77.2 0.0 copy-start.10
  77.2 1.2 copy-done.10
  78.4 5.7 %shard_map.88 = (f32[8,256,128]{2,1,0:T(8,128)S(1)}, f32[8,256,128]{2,1,0:T(8,128)S(1)}, f32[8,256,128]{2,1,0:T(8,128)S(1)}) custom-call(s32[4]{0:T(128)S(1)} %copy-done.3, s32[4,8]{1,0:T(4,128)S(1)} %copy-done.2, s32[4,8]{1,0:T(4,128)S(1)} %copy-done.6, s32[4,8]{1,0:T(4,128)S(1)} %copy-done.8, s32[4,8]{1,0:T(4,128)S(1)} %collective-permute-done.2.refs_4_, ...), custom_call_target="tpu_custom_call" | custom-call | flops 2000000000 | bytes 8000000 | tf_op jit(solution)/shard_map/pallas_call | solution.py:192
  84.2 0.1 collective-permute-start.8
  84.2 0.1 collective-permute-start.10
  84.3 30.4 %collective-permute-done.8.refs_6_ = f32[8,256,128]{2,1,0:T(8,128)S(1)} collective-permute-done((f32[8,256,128]{2,1,0:T(8,128)S(1)}, f32[8,256,128]{2,1,0:T(8,128)S(1)}, u32[]{:S(2)}, u32[]{:S(2)}) %collective-permute-start.8) | collective-permute-done | bytes 1048608 | tf_op jit(solution)/shard_map/ppermute | solution.py:212
  114.7 5.7 %shard_map.89 = (f32[8,256,128]{2,1,0:T(8,128)}, f32[8,256,128]{2,1,0:T(8,128)S(1)}) custom-call(s32[4]{0:T(128)S(1)} %copy-done.3, s32[4,8]{1,0:T(4,128)S(1)} %copy-done.2, s32[4,8]{1,0:T(4,128)S(1)} %copy-done.6, s32[4,8,256]{2,1,0:T(8,128)S(1)} %copy-done.5, s32[4,8,4,256]{3,2,1,0:T(4,128)S(1)} %copy-done.4, ...), custom_call_target="tpu_custom_call" | custom-call | flops 2000000000 | bytes 8000000 | tf_op jit(solution)/shard_map/pallas_call | solution.py:192
  120.4 2.1 %collective-permute-start.1 = (s32[4,8]{1,0:T(4,128)S(1)}, s32[4,8]{1,0:T(4,128)S(1)}, u32[]{:S(2)}, u32[]{:S(2)}) collective-permute-start(s32[4,8]{1,0:T(4,128)S(1)} %copy-done.2), channel_id=1, source_target_pairs={{0,8},{1,9},{2,10},{3,11},{4,12},{5,13},{6,14},{7,15},{8,16},{9,17... | collective-permute-start | bytes 392 | tf_op jit(solution)/shard_map/ppermute | solution.py:212
  122.5 12.1 %collective-permute-done.1.group = s32[4,8]{1,0:T(4,128)S(1)} collective-permute-done((s32[4,8]{1,0:T(4,128)S(1)}, s32[4,8]{1,0:T(4,128)S(1)}, u32[]{:S(2)}, u32[]{:S(2)}) %collective-permute-start.1) | collective-permute-done | bytes 160 | tf_op jit(solution)/shard_map/ppermute | solution.py:212
  134.6 0.0 collective-permute-done.10.minus
  134.6 0.0 collective-permute-done.9.plus
  134.6 2.1 %shard_map.90 = f32[16,256,128]{2,1,0:T(8,128)} custom-call(s32[4,8]{1,0:T(4,128)S(1)} %collective-permute-done.1.group, f32[8,256,128]{2,1,0:T(8,128)S(1)} %collective-permute-done.9.plus, f32[8,256,128]{2,1,0:T(8,128)S(1)} %collective-permute-done.10.minus), custom_call_target="tpu_custom_call" | custom-call | flops 2000000000 | bytes 8000000 | tf_op jit(solution)/shard_map/pallas_call | solution.py:192
  (20 shorter events, 0.0 us)
Async XLA Ops:
  1.4 7.3 %copy-start = (s32[4,8]{1,0:T(4,128)}, s32[4,8]{1,0:T(4,128)S(1)}, u32[]{:S(2)}) copy-start(s32[4,8]{1,0:T(4,128)S(1)} %fusion.vert.refs_1_) | copy-start | bytes 388
  1.4 7.3 %collective-permute-start = (s32[4,8]{1,0:T(4,128)S(1)}, s32[4,8]{1,0:T(4,128)S(1)}, u32[]{:S(2)}, u32[]{:S(2)}) collective-permute-start(s32[4,8]{1,0:T(4,128)S(1)} %fusion.vert.refs_1_), channel_id=1, source_target_pairs={{0,7},{1,0},{2,1},{3,2},{4,3},{5,4},{6,5},{7,6},{8,15},{9,8},{10,9... | collective-permute-start | bytes 392 | tf_op jit(solution)/shard_map/ppermute | solution.py:212
  8.7 0.6 copy-start.7
  9.3 37.9 %copy-start.3 = (s32[4]{0:T(128)S(1)}, s32[4]{0:T(128)}, u32[]{:S(2)}) copy-start(s32[4]{0:T(128)} %refs_0_.5) | copy-start | bytes 52
  9.3 37.9 %copy-start.4 = (s32[4,8,4,256]{3,2,1,0:T(4,128)S(1)}, s32[4,8,4,256]{3,2,1,0:T(4,128)}, u32[]{:S(2)}) copy-start(s32[4,8,4,256]{3,2,1,0:T(4,128)} %refs_4_.3) | copy-start | bytes 393220
  9.3 37.9 %copy-start.5 = (s32[4,8,256]{2,1,0:T(8,128)S(1)}, s32[4,8,256]{2,1,0:T(8,128)}, u32[]{:S(2)}) copy-start(s32[4,8,256]{2,1,0:T(8,128)} %refs_3_.3) | copy-start | bytes 98308
  9.3 37.9 %copy-start.6 = (s32[4,8]{1,0:T(4,128)S(1)}, s32[4,8]{1,0:T(4,128)}, u32[]{:S(2)}) copy-start(s32[4,8]{1,0:T(4,128)} %refs_2_.5) | copy-start | bytes 388
  18.2 29.0 %collective-permute-start.3 = (f32[8,256,128]{2,1,0:T(8,128)}, f32[8,256,128]{2,1,0:T(8,128)S(1)}, u32[]{:S(2)}, u32[]{:S(2)}) collective-permute-start(f32[8,256,128]{2,1,0:T(8,128)} %get-tuple-element.18), channel_id=1, source_target_pairs={{0,1},{1,2},{2,3},{3,4},{4,5},{5,6},{6,7},{7,0},{8,9},{9,10},{10,1... | collective-permute-start | bytes 3145736 | tf_op jit(solution)/shard_map/ppermute | solution.py:212
  18.2 58.9 %collective-permute-start.7 = (f32[8,256,128]{2,1,0:T(8,128)}, f32[8,256,128]{2,1,0:T(8,128)S(1)}, u32[]{:S(2)}, u32[]{:S(2)}) collective-permute-start(f32[8,256,128]{2,1,0:T(8,128)} %get-tuple-element.22), channel_id=1, source_target_pairs={{0,2},{1,3},{2,4},{3,5},{4,6},{5,7},{6,0},{7,1},{8,10},{9,11},{10,... | collective-permute-start | bytes 3145736 | tf_op jit(solution)/shard_map/ppermute | solution.py:212
  47.2 0.7 copy-start.1
  47.9 1.2 copy-start.11
  49.1 16.8 %copy-start.2 = (s32[4,8]{1,0:T(4,128)S(1)}, s32[4,8]{1,0:T(4,128)}, u32[]{:S(2)}) copy-start(s32[4,8]{1,0:T(4,128)} %copy-done) | copy-start | bytes 388
  49.1 28.1 %copy-start.8 = (s32[4,8]{1,0:T(4,128)S(1)}, s32[4,8]{1,0:T(4,128)}, u32[]{:S(2)}) copy-start(s32[4,8]{1,0:T(4,128)} %copy-done.7) | copy-start | bytes 388
  52.9 1.0 copy-start.9
  53.9 10.1 %collective-permute-start.5 = (f32[4,256,128]{2,1,0:T(8,128)S(1)}, f32[4,256,128]{2,1,0:T(8,128)S(1)}, u32[]{:S(2)}, u32[]{:S(2)}) collective-permute-start(f32[4,256,128]{2,1,0:T(8,128)S(1)} %get-tuple-element.21), channel_id=1, source_target_pairs={{0,1},{1,0},{2,3},{3,2},{4,5},{5,4},{6,7},{7,6},{8,9},{9,8},{10,11... | collective-permute-start | bytes 1572872 | tf_op jit(solution)/shard_map/ppermute | solution.py:212
  53.9 23.3 %collective-permute-start.4 = (f32[4,256,128]{2,1,0:T(8,128)S(1)}, f32[4,256,128]{2,1,0:T(8,128)S(1)}, u32[]{:S(2)}, u32[]{:S(2)}) collective-permute-start(f32[4,256,128]{2,1,0:T(8,128)S(1)} %get-tuple-element.20), channel_id=1, source_target_pairs={{0,1},{1,2},{2,3},{3,4},{4,5},{5,6},{6,7},{7,0},{8,9},{9,10},{10,1... | collective-permute-start | bytes 1572872 | tf_op jit(solution)/shard_map/ppermute | solution.py:212
  63.9 13.2 %collective-permute-start.6 = (f32[4,256,128]{2,1,0:T(8,128)S(1)}, f32[4,256,128]{2,1,0:T(8,128)}, u32[]{:S(2)}, u32[]{:S(2)}) collective-permute-start(f32[4,256,128]{2,1,0:T(8,128)S(1)} %collective-permute-done.5.refs_10_), channel_id=1, source_target_pairs={{0,2},{2,4},{4,6},{6,0},{8,10},{10,12},{12,14},{14,8},{16,18},{18,... | collective-permute-start | bytes 1572872 | tf_op jit(solution)/shard_map/ppermute | solution.py:212
  65.9 11.3 %collective-permute-start.2 = (s32[4,8]{1,0:T(4,128)S(1)}, s32[4,8]{1,0:T(4,128)S(1)}, u32[]{:S(2)}, u32[]{:S(2)}) collective-permute-start(s32[4,8]{1,0:T(4,128)S(1)} %copy-done.2), channel_id=1, source_target_pairs={{0,1},{1,2},{2,3},{3,4},{4,5},{5,6},{6,7},{7,0},{8,9},{9,10},{10,1... | collective-permute-start | bytes 392 | tf_op jit(solution)/shard_map/ppermute | solution.py:212
  77.2 1.2 copy-start.10
  84.2 30.5 %collective-permute-start.8 = (f32[8,256,128]{2,1,0:T(8,128)S(1)}, f32[8,256,128]{2,1,0:T(8,128)S(1)}, u32[]{:S(2)}, u32[]{:S(2)}) collective-permute-start(f32[8,256,128]{2,1,0:T(8,128)S(1)} %get-tuple-element.24), channel_id=1, source_target_pairs={{0,1},{1,2},{2,3},{3,4},{4,5},{5,6},{6,7},{7,0},{8,9},{9,10},{10,1... | collective-permute-start | bytes 3145736 | tf_op jit(solution)/shard_map/ppermute | solution.py:212
  84.2 50.4 %collective-permute-start.10 = (f32[8,256,128]{2,1,0:T(8,128)S(1)}, f32[8,256,128]{2,1,0:T(8,128)S(1)}, u32[]{:S(2)}, u32[]{:S(2)}) collective-permute-start(f32[8,256,128]{2,1,0:T(8,128)S(1)} %get-tuple-element.26), channel_id=1, source_target_pairs={{0,9},{1,10},{2,11},{3,12},{4,13},{5,14},{6,15},{7,8},{8,17},{9,18... | collective-permute-start | bytes 3145736 | tf_op jit(solution)/shard_map/ppermute | solution.py:212
  120.4 14.3 %collective-permute-start.9 = (f32[8,256,128]{2,1,0:T(8,128)S(1)}, f32[8,256,128]{2,1,0:T(8,128)S(1)}, u32[]{:S(2)}, u32[]{:S(2)}) collective-permute-start(f32[8,256,128]{2,1,0:T(8,128)S(1)} %get-tuple-element.25), channel_id=1, source_target_pairs={{0,8},{1,9},{2,10},{3,11},{4,12},{5,13},{6,14},{7,15},{8,16},{9,17... | collective-permute-start | bytes 3145736 | tf_op jit(solution)/shard_map/ppermute | solution.py:212
  120.4 14.2 %collective-permute-start.1 = (s32[4,8]{1,0:T(4,128)S(1)}, s32[4,8]{1,0:T(4,128)S(1)}, u32[]{:S(2)}, u32[]{:S(2)}) collective-permute-start(s32[4,8]{1,0:T(4,128)S(1)} %copy-done.2), channel_id=1, source_target_pairs={{0,8},{1,9},{2,10},{3,11},{4,12},{5,13},{6,14},{7,15},{8,16},{9,17... | collective-permute-start | bytes 392 | tf_op jit(solution)/shard_map/ppermute | solution.py:212

commit v3 on v2

--- a/solution.py
+++ b/solution.py
@@ -77,12 +77,12 @@
     lax.fori_loop(0, (count + group - 1) // group, slot_group, 0)
 
 
-def split(v, order, plus, minus):
-    near = plus.shape[0]
-    for k in range(near):
-        plus[k] = v[order[k]]
-    for k in range(minus.shape[0]):
-        minus[k] = v[order[near + k]]
+def split(v, order, outs):
+    start = 0
+    for out in outs:
+        for k in range(out.shape[0]):
+            out[k] = v[order[start + k]]
+        start += out.shape[0]
 
 
 def first_kernel(
@@ -111,13 +111,13 @@
         0, count[s], lambda t: vert[s, t], lambda t: context_tiles[s, t], positives, negatives,
         v_old, v_new, c_old, c_new,
     )
-    split(v_new, order, plus, minus)
+    split(v_new, order, (plus, minus))
 
 
 def merge_kernel(s, *refs):
     count, vert, context_tiles, right, left, odd = refs[:6]
     positives, negatives, c_old, direct, swapped, relayed, minus_in = refs[6:13]
-    c_new, plus, minus, v_old, v_new, order, mark = refs[13:]
+    c_new, plus, *minus, v_old, v_new, order, mark = refs[13:]
     tiles, near, slots = v_old.shape[0], plus.shape[0], vert.shape[1]
     first = direct.shape[0]
     ordered(tiles, slots, lambda t: left[s - 1, t], order, None, mark)
@@ -147,7 +147,7 @@
         v_old, v_new, c_old, c_new,
     )
     ordered(tiles, slots, lambda t: right[s + 1, t], order, None, mark)
-    split(v_new, order, plus, minus)
+    split(v_new, order, (plus, *minus))
 
 
 def near_kernel(s, tiles, *refs):
@@ -166,14 +166,12 @@
         start += out.shape[0]
 
 
-def final_kernel(s, group, plus, minus, out, order, mark, sems):
-    near, tiles = plus.shape[0], out.shape[0]
+def final_kernel(s, group, plus, early, minus, out, order, mark, sems):
+    tiles = out.shape[0]
     ordered(tiles, group.shape[1], lambda t: group[s, t], order, None, mark)
+    sources = [part.at[k] for part in (plus, early, minus) for k in range(part.shape[0])]
     copies = [
-        pltpu.make_async_copy(
-            plus.at[k] if k < near else minus.at[k - near], out.at[order[k]], sems.at[k]
-        )
-        for k in range(tiles)
+        pltpu.make_async_copy(sources[k], out.at[order[k]], sems.at[k]) for k in range(tiles)
     ]
     for copy in copies:
         copy.start()
@@ -261,13 +259,22 @@
     for s in range(steps):
         if s % 2 == 0:
             if s > 0:
-                c, plus, minus = call(
+                more = s + 2 < steps
+                far_shapes = (far_shape,) if more else tuple(
+                    jax.ShapeDtypeStruct((size, TILE, width), f32)
+                    for size in (far // 2, far - far // 2)
+                )
+                c, plus, *minuses = call(
                     part(merge_kernel, s), lists + [right, left, odd],
                     rows + [c, direct, swapped, relayed, minus],
-                    (c_shape, near_shape, far_shape), buffers + marks,
+                    (c_shape, near_shape) + far_shapes, buffers + marks,
                 )
             plus = moved(plus, 0, 1)
+            if s > 0:
+                minus = minuses[-1]
             minus = moved(minus, 0, 2) if s + 2 < steps else moved(minus, 1, 1)
+            if s > 0 and s + 2 >= steps:
+                early = moved(minuses[0], 1, 1)
             if s == 0:
                 left = moved(late, 0, 1)
                 group = moved(late, 1, 0)
@@ -285,7 +292,7 @@
             else:
                 plus = moved(parts[0], 1, 0)
     v = call(
-        part(final_kernel, steps - 1), [group], [plus, minus], v_shape,
+        part(final_kernel, steps - 1), [group], [plus, early, minus], v_shape,
         marks + [pltpu.SemaphoreType.DMA((tiles,))], out_space=HBM,
     )
     return v.reshape(vertex.shape), c.reshape(context.shape)

time: 138 us -> 145 us (1.051)
  waiting for transfers between devices: 91.2 us -> 98.9 us
    ppermute x11 -> x12, waiting for transfers between devices: 91.2 us -> 98.9 us  [moved(): return lax.ppermute(block, ('outer', 'inner'), route)]
    ppermute x11 -> x12, starting transfers between devices: 13.2 us -> 13.1 us  [moved(): return lax.ppermute(block, ('outer', 'inner'), route)]
  transfers between devices with their start and end apart: 11 -> 12, of which waited for: 6 -> 7; matrix products, arithmetic and copies ran while one was open for 0% -> 0% of each run, Pallas kernels for 7% -> 3%
where the time goes in v3:
time: 145 us; the launch traced here: 144 us
  waiting for transfers between devices  98.9 us (68%)
  Pallas kernels  26.1 us (18%)
  starting transfers between devices  13.1 us (9%)
  local copies, waits for them, and re-layouts  4.69 us (3%)
    ppermute x12, waiting for transfers between devices, moved(): return lax.ppermute(block, ('outer', 'inner'), route)  98.9 us
    pallas_call x5, Pallas kernels, call(): pl.pallas_call(kernel, out_shape=outs, in_specs=[SMEM] * len(scalars) + [...  26.1 us
    ppermute x12, starting transfers between devices, moved(): return lax.ppermute(block, ('outer', 'inner'), route)  13.1 us
    unnamed x24, local copies, waits for them, and re-layouts  4.69 us
  transfers between devices with their start and end apart: 12, of which 7 were waited for; matrix products, arithmetic and copies ran while one was open for 0% of the time, Pallas kernels for 3%

profile of v3, /device:TPU:0, one launch (start us, length us, event | category | flops | bytes accessed | tf_op | source)
XLA Modules:
  0.0 144.3 jit_solution(7497272431742917842)
XLA Ops:
  0.6 0.8 fusion.vert.refs_1_
  1.4 6.0 %collective-permute-start = (s32[4,8]{1,0:T(4,128)S(1)}, s32[4,8]{1,0:T(4,128)S(1)}, u32[]{:S(2)}, u32[]{:S(2)}) collective-permute-start(s32[4,8]{1,0:T(4,128)S(1)} %fusion.vert.refs_1_), channel_id=1, source_target_pairs={{0,7},{1,0},{2,1},{3,2},{4,3},{5,4},{6,5},{7,6},{8,15},{9,8},{10,9... | collective-permute-start | bytes 392 | tf_op jit(solution)/shard_map/ppermute | solution.py:210
  7.4 1.3 collective-permute-done.right.refs_3_
  8.7 0.6 copy-done.7
  9.3 8.8 %shard_map.86 = (f32[8,256,128]{2,1,0:T(8,128)}, f32[8,256,128]{2,1,0:T(8,128)}, f32[8,256,128]{2,1,0:T(8,128)}) custom-call(s32[4]{0:T(128)} %refs_0_.5, s32[4,8]{1,0:T(4,128)} %copy-done, s32[4,8]{1,0:T(4,128)} %refs_2_.5, s32[4,8]{1,0:T(4,128)} %copy-done.7, s32[4,8,256]{2,1,0:T(8,128)} %refs_3_.3, s32[4,8,4,256]{3,2,1,0:T(4,128)} %refs_4_.3, ...), custom_call_target="tpu_custom_call" | custom-call | flops 2000000000 | bytes 8000000 | tf_op jit(solution)/shard_map/pallas_call | solution.py:190
  18.2 0.1 collective-permute-start.3
  18.2 0.1 collective-permute-start.7
  18.3 28.9 %collective-permute-done.3.refs_6_ = f32[8,256,128]{2,1,0:T(8,128)S(1)} collective-permute-done((f32[8,256,128]{2,1,0:T(8,128)}, f32[8,256,128]{2,1,0:T(8,128)S(1)}, u32[]{:S(2)}, u32[]{:S(2)}) %collective-permute-start.3) | collective-permute-done | bytes 1048608 | tf_op jit(solution)/shard_map/ppermute | solution.py:210
  47.2 0.7 copy-done.1
  47.9 1.2 copy-done.11
  49.1 3.8 %shard_map.87 = (f32[8,256,128]{2,1,0:T(8,128)S(1)}, f32[4,256,128]{2,1,0:T(8,128)S(1)}, f32[4,256,128]{2,1,0:T(8,128)S(1)}) custom-call(s32[4]{0:T(128)S(1)} %copy-done.3, s32[4,8]{1,0:T(4,128)S(1)} %copy-done.1, s32[4,8]{1,0:T(4,128)S(1)} %copy-done.6, s32[4,8,256]{2,1,0:T(8,128)S(1)} %copy-done.5, s32[4,8,4,256]{3,2,1,0:T(4,128)S(1)} %copy-done.4, ...), custom_call_target="tpu_custom_call" | custom-call | flops 2000000000 | bytes 8000000 | tf_op jit(solution)/shard_map/pallas_call | solution.py:190
  52.9 0.0 copy-start.9
  52.9 1.0 copy-done.9
  53.9 0.0 collective-permute-start.5
  53.9 2.0 %collective-permute-start.4 = (f32[4,256,128]{2,1,0:T(8,128)S(1)}, f32[4,256,128]{2,1,0:T(8,128)S(1)}, u32[]{:S(2)}, u32[]{:S(2)}) collective-permute-start(f32[4,256,128]{2,1,0:T(8,128)S(1)} %get-tuple-element.21), channel_id=1, source_target_pairs={{0,1},{1,2},{2,3},{3,4},{4,5},{5,6},{6,7},{7,0},{8,9},{9,10},{10,1... | collective-permute-start | bytes 1572872 | tf_op jit(solution)/shard_map/ppermute | solution.py:210
  55.9 8.1 %collective-permute-done.5.refs_10_ = f32[4,256,128]{2,1,0:T(8,128)S(1)} collective-permute-done((f32[4,256,128]{2,1,0:T(8,128)S(1)}, f32[4,256,128]{2,1,0:T(8,128)S(1)}, u32[]{:S(2)}, u32[]{:S(2)}) %collective-permute-start.5) | collective-permute-done | bytes 524320 | tf_op jit(solution)/shard_map/ppermute | solution.py:210
  64.0 1.9 %collective-permute-start.6 = (f32[4,256,128]{2,1,0:T(8,128)S(1)}, f32[4,256,128]{2,1,0:T(8,128)}, u32[]{:S(2)}, u32[]{:S(2)}) collective-permute-start(f32[4,256,128]{2,1,0:T(8,128)S(1)} %collective-permute-done.5.refs_10_), channel_id=1, source_target_pairs={{0,2},{2,4},{4,6},{6,0},{8,10},{10,12},{12,14},{14,8},{16,18},{18,... | collective-permute-start | bytes 1572872 | tf_op jit(solution)/shard_map/ppermute | solution.py:210
  65.9 0.8 collective-permute-start.2
  66.7 10.5 %collective-permute-done.2.refs_4_ = s32[4,8]{1,0:T(4,128)S(1)} collective-permute-done((s32[4,8]{1,0:T(4,128)S(1)}, s32[4,8]{1,0:T(4,128)S(1)}, u32[]{:S(2)}, u32[]{:S(2)}) %collective-permute-start.2) | collective-permute-done | bytes 160 | tf_op jit(solution)/shard_map/ppermute | solution.py:210
  77.2 0.0 collective-permute-done.7.refs_12_
  77.2 0.0 collective-permute-done.4.refs_9_
  77.2 0.0 collective-permute-done.6.refs_11_
  77.2 0.0 copy-start.10
  77.2 1.2 copy-done.10
  78.4 5.7 %shard_map.88 = (f32[8,256,128]{2,1,0:T(8,128)S(1)}, f32[8,256,128]{2,1,0:T(8,128)S(1)}, f32[4,256,128]{2,1,0:T(8,128)S(1)}, f32[4,256,128]{2,1,0:T(8,128)S(1)}) custom-call(s32[4]{0:T(128)S(1)} %copy-done.3, s32[4,8]{1,0:T(4,128)S(1)} %copy-done.2, s32[4,8]{1,0:T(4,128)S(1)} %copy-done.6, s32[4,8]{1,0:T(4,128)S(1)} %copy-done.8, ...), custom_call_target="tpu_custom_call" | custom-call | flops 2000000000 | bytes 8000000 | tf_op jit(solution)/shard_map/pallas_call | solution.py:190
  84.2 0.1 collective-permute-start.8
  84.2 24.1 %collective-permute-done.8.refs_6_ = f32[8,256,128]{2,1,0:T(8,128)S(1)} collective-permute-done((f32[8,256,128]{2,1,0:T(8,128)S(1)}, f32[8,256,128]{2,1,0:T(8,128)S(1)}, u32[]{:S(2)}, u32[]{:S(2)}) %collective-permute-start.8) | collective-permute-done | bytes 1048608 | tf_op jit(solution)/shard_map/ppermute | solution.py:210
  108.3 5.7 %shard_map.89 = (f32[8,256,128]{2,1,0:T(8,128)}, f32[8,256,128]{2,1,0:T(8,128)S(1)}) custom-call(s32[4]{0:T(128)S(1)} %copy-done.3, s32[4,8]{1,0:T(4,128)S(1)} %copy-done.2, s32[4,8]{1,0:T(4,128)S(1)} %copy-done.6, s32[4,8,256]{2,1,0:T(8,128)S(1)} %copy-done.5, s32[4,8,4,256]{3,2,1,0:T(4,128)S(1)} %copy-done.4, ...), custom_call_target="tpu_custom_call" | custom-call | flops 2000000000 | bytes 8000000 | tf_op jit(solution)/shard_map/pallas_call | solution.py:190
  114.1 2.1 %collective-permute-start.1 = (s32[4,8]{1,0:T(4,128)S(1)}, s32[4,8]{1,0:T(4,128)S(1)}, u32[]{:S(2)}, u32[]{:S(2)}) collective-permute-start(s32[4,8]{1,0:T(4,128)S(1)} %copy-done.2), channel_id=1, source_target_pairs={{0,8},{1,9},{2,10},{3,11},{4,12},{5,13},{6,14},{7,15},{8,16},{9,17... | collective-permute-start | bytes 392 | tf_op jit(solution)/shard_map/ppermute | solution.py:210
  116.2 23.4 %collective-permute-done.1.group = s32[4,8]{1,0:T(4,128)S(1)} collective-permute-done((s32[4,8]{1,0:T(4,128)S(1)}, s32[4,8]{1,0:T(4,128)S(1)}, u32[]{:S(2)}, u32[]{:S(2)}) %collective-permute-start.1) | collective-permute-done | bytes 160 | tf_op jit(solution)/shard_map/ppermute | solution.py:210
  139.5 2.7 %collective-permute-done.11.minus = f32[4,256,128]{2,1,0:T(8,128)S(1)} collective-permute-done((f32[4,256,128]{2,1,0:T(8,128)S(1)}, f32[4,256,128]{2,1,0:T(8,128)S(1)}, u32[]{:S(2)}, u32[]{:S(2)}) %collective-permute-start.11) | collective-permute-done | bytes 524320 | tf_op jit(solution)/shard_map/ppermute | solution.py:210
  142.3 2.1 %shard_map.90 = f32[16,256,128]{2,1,0:T(8,128)} custom-call(s32[4,8]{1,0:T(4,128)S(1)} %collective-permute-done.1.group, f32[8,256,128]{2,1,0:T(8,128)S(1)} %collective-permute-done.9.plus, f32[4,256,128]{2,1,0:T(8,128)S(1)} %collective-permute-done.10.early, f32[4,256,128]{2,1,0:T(8,128)S(1)} %collective-permute-done.11.minus), custom_call_target="tpu_custom_call" | custom-call | flops 2000000000 | bytes 8000000 | tf_op jit(solution)/shard_map/pallas_call | solution.py:190
  (22 shorter events, 0.0 us)
Async XLA Ops:
  1.4 7.3 %copy-start = (s32[4,8]{1,0:T(4,128)}, s32[4,8]{1,0:T(4,128)S(1)}, u32[]{:S(2)}) copy-start(s32[4,8]{1,0:T(4,128)S(1)} %fusion.vert.refs_1_) | copy-start | bytes 388
  1.4 7.3 %collective-permute-start = (s32[4,8]{1,0:T(4,128)S(1)}, s32[4,8]{1,0:T(4,128)S(1)}, u32[]{:S(2)}, u32[]{:S(2)}) collective-permute-start(s32[4,8]{1,0:T(4,128)S(1)} %fusion.vert.refs_1_), channel_id=1, source_target_pairs={{0,7},{1,0},{2,1},{3,2},{4,3},{5,4},{6,5},{7,6},{8,15},{9,8},{10,9... | collective-permute-start | bytes 392 | tf_op jit(solution)/shard_map/ppermute | solution.py:210
  8.7 0.6 copy-start.7
  9.3 37.9 %copy-start.3 = (s32[4]{0:T(128)S(1)}, s32[4]{0:T(128)}, u32[]{:S(2)}) copy-start(s32[4]{0:T(128)} %refs_0_.5) | copy-start | bytes 52
  9.3 37.9 %copy-start.4 = (s32[4,8,4,256]{3,2,1,0:T(4,128)S(1)}, s32[4,8,4,256]{3,2,1,0:T(4,128)}, u32[]{:S(2)}) copy-start(s32[4,8,4,256]{3,2,1,0:T(4,128)} %refs_4_.3) | copy-start | bytes 393220
  9.3 37.9 %copy-start.5 = (s32[4,8,256]{2,1,0:T(8,128)S(1)}, s32[4,8,256]{2,1,0:T(8,128)}, u32[]{:S(2)}) copy-start(s32[4,8,256]{2,1,0:T(8,128)} %refs_3_.3) | copy-start | bytes 98308
  9.3 37.9 %copy-start.6 = (s32[4,8]{1,0:T(4,128)S(1)}, s32[4,8]{1,0:T(4,128)}, u32[]{:S(2)}) copy-start(s32[4,8]{1,0:T(4,128)} %refs_2_.5) | copy-start | bytes 388
  18.2 29.0 %collective-permute-start.3 = (f32[8,256,128]{2,1,0:T(8,128)}, f32[8,256,128]{2,1,0:T(8,128)S(1)}, u32[]{:S(2)}, u32[]{:S(2)}) collective-permute-start(f32[8,256,128]{2,1,0:T(8,128)} %get-tuple-element.19), channel_id=1, source_target_pairs={{0,1},{1,2},{2,3},{3,4},{4,5},{5,6},{6,7},{7,0},{8,9},{9,10},{10,1... | collective-permute-start | bytes 3145736 | tf_op jit(solution)/shard_map/ppermute | solution.py:210
  18.2 58.9 %collective-permute-start.7 = (f32[8,256,128]{2,1,0:T(8,128)}, f32[8,256,128]{2,1,0:T(8,128)S(1)}, u32[]{:S(2)}, u32[]{:S(2)}) collective-permute-start(f32[8,256,128]{2,1,0:T(8,128)} %get-tuple-element.23), channel_id=1, source_target_pairs={{0,2},{1,3},{2,4},{3,5},{4,6},{5,7},{6,0},{7,1},{8,10},{9,11},{10,... | collective-permute-start | bytes 3145736 | tf_op jit(solution)/shard_map/ppermute | solution.py:210
  47.2 0.7 copy-start.1
  47.9 1.2 copy-start.11
  49.1 16.8 %copy-start.2 = (s32[4,8]{1,0:T(4,128)S(1)}, s32[4,8]{1,0:T(4,128)}, u32[]{:S(2)}) copy-start(s32[4,8]{1,0:T(4,128)} %copy-done) | copy-start | bytes 388
  49.1 28.1 %copy-start.8 = (s32[4,8]{1,0:T(4,128)S(1)}, s32[4,8]{1,0:T(4,128)}, u32[]{:S(2)}) copy-start(s32[4,8]{1,0:T(4,128)} %copy-done.7) | copy-start | bytes 388
  52.9 1.0 copy-start.9
  53.9 10.1 %collective-permute-start.5 = (f32[4,256,128]{2,1,0:T(8,128)S(1)}, f32[4,256,128]{2,1,0:T(8,128)S(1)}, u32[]{:S(2)}, u32[]{:S(2)}) collective-permute-start(f32[4,256,128]{2,1,0:T(8,128)S(1)} %get-tuple-element.22), channel_id=1, source_target_pairs={{0,1},{1,0},{2,3},{3,2},{4,5},{5,4},{6,7},{7,6},{8,9},{9,8},{10,11... | collective-permute-start | bytes 1572872 | tf_op jit(solution)/shard_map/ppermute | solution.py:210
  53.9 23.3 %collective-permute-start.4 = (f32[4,256,128]{2,1,0:T(8,128)S(1)}, f32[4,256,128]{2,1,0:T(8,128)S(1)}, u32[]{:S(2)}, u32[]{:S(2)}) collective-permute-start(f32[4,256,128]{2,1,0:T(8,128)S(1)} %get-tuple-element.21), channel_id=1, source_target_pairs={{0,1},{1,2},{2,3},{3,4},{4,5},{5,6},{6,7},{7,0},{8,9},{9,10},{10,1... | collective-permute-start | bytes 1572872 | tf_op jit(solution)/shard_map/ppermute | solution.py:210
  64.0 13.2 %collective-permute-start.6 = (f32[4,256,128]{2,1,0:T(8,128)S(1)}, f32[4,256,128]{2,1,0:T(8,128)}, u32[]{:S(2)}, u32[]{:S(2)}) collective-permute-start(f32[4,256,128]{2,1,0:T(8,128)S(1)} %collective-permute-done.5.refs_10_), channel_id=1, source_target_pairs={{0,2},{2,4},{4,6},{6,0},{8,10},{10,12},{12,14},{14,8},{16,18},{18,... | collective-permute-start | bytes 1572872 | tf_op jit(solution)/shard_map/ppermute | solution.py:210
  65.9 11.3 %collective-permute-start.2 = (s32[4,8]{1,0:T(4,128)S(1)}, s32[4,8]{1,0:T(4,128)S(1)}, u32[]{:S(2)}, u32[]{:S(2)}) collective-permute-start(s32[4,8]{1,0:T(4,128)S(1)} %copy-done.2), channel_id=1, source_target_pairs={{0,1},{1,2},{2,3},{3,4},{4,5},{5,6},{6,7},{7,0},{8,9},{9,10},{10,1... | collective-permute-start | bytes 392 | tf_op jit(solution)/shard_map/ppermute | solution.py:210
  77.2 1.2 copy-start.10
  84.2 24.2 %collective-permute-start.8 = (f32[8,256,128]{2,1,0:T(8,128)S(1)}, f32[8,256,128]{2,1,0:T(8,128)S(1)}, u32[]{:S(2)}, u32[]{:S(2)}) collective-permute-start(f32[8,256,128]{2,1,0:T(8,128)S(1)} %get-tuple-element.25), channel_id=1, source_target_pairs={{0,1},{1,2},{2,3},{3,4},{4,5},{5,6},{6,7},{7,0},{8,9},{9,10},{10,1... | collective-permute-start | bytes 3145736 | tf_op jit(solution)/shard_map/ppermute | solution.py:210
  114.0 28.2 %collective-permute-start.9 = (f32[8,256,128]{2,1,0:T(8,128)S(1)}, f32[8,256,128]{2,1,0:T(8,128)S(1)}, u32[]{:S(2)}, u32[]{:S(2)}) collective-permute-start(f32[8,256,128]{2,1,0:T(8,128)S(1)} %get-tuple-element.26), channel_id=1, source_target_pairs={{0,8},{1,9},{2,10},{3,11},{4,12},{5,13},{6,14},{7,15},{8,16},{9,17... | collective-permute-start | bytes 3145736 | tf_op jit(solution)/shard_map/ppermute | solution.py:210
  114.0 25.5 %collective-permute-start.10 = (f32[4,256,128]{2,1,0:T(8,128)S(1)}, f32[4,256,128]{2,1,0:T(8,128)S(1)}, u32[]{:S(2)}, u32[]{:S(2)}) collective-permute-start(f32[4,256,128]{2,1,0:T(8,128)S(1)} %get-tuple-element.27), channel_id=1, source_target_pairs={{0,9},{1,10},{2,11},{3,12},{4,13},{5,14},{6,15},{7,8},{8,17},{9,18... | collective-permute-start | bytes 1572872 | tf_op jit(solution)/shard_map/ppermute | solution.py:210
  114.1 28.2 %collective-permute-start.11 = (f32[4,256,128]{2,1,0:T(8,128)S(1)}, f32[4,256,128]{2,1,0:T(8,128)S(1)}, u32[]{:S(2)}, u32[]{:S(2)}) collective-permute-start(f32[4,256,128]{2,1,0:T(8,128)S(1)} %get-tuple-element.28), channel_id=1, source_target_pairs={{0,9},{1,10},{2,11},{3,12},{4,13},{5,14},{6,15},{7,8},{8,17},{9,18... | collective-permute-start | bytes 1572872 | tf_op jit(solution)/shard_map/ppermute | solution.py:210
  114.1 25.5 %collective-permute-start.1 = (s32[4,8]{1,0:T(4,128)S(1)}, s32[4,8]{1,0:T(4,128)S(1)}, u32[]{:S(2)}, u32[]{:S(2)}) collective-permute-start(s32[4,8]{1,0:T(4,128)S(1)} %copy-done.2), channel_id=1, source_target_pairs={{0,8},{1,9},{2,10},{3,11},{4,12},{5,13},{6,14},{7,15},{8,16},{9,17... | collective-permute-start | bytes 392 | tf_op jit(solution)/shard_map/ppermute | solution.py:210
